TPU v7x, 32 devices: a whole 2x2x4 slice. The times are simulated.
32 devices in a mesh: gx: 4 (over x, core), gy: 4 (over z), gz: 2 (over y).
Axes of the slice: x: 2, y: 2, z: 4, core: 2. Of those that a mesh axis runs over, the one named last changes fastest.
Arguments:
- displacement: float32 [3, 32, 32, 256], P(None, 'gx', 'gy', 'gz'), may hold values from -0.25 to 0.25
- bond_intact: int32 [61, 32, 32, 256], P(None, 'gx', 'gy', 'gz'), may hold values 0 or 1
Outputs:
- force: float32 [3, 32, 32, 256], P(None, 'gx', 'gy', 'gz')
- dilatation: float32 [32, 32, 256], P('gx', 'gy', 'gz')
All inputs are finite; a program needn't handle non-finite values. No bound on the sum of `bond_intact` on one device may be relied on, other than what follows from the above.
Results may differ from a plain program's by a relative error of at most 0.000063.
Values sent between devices are 32-bit elements; how exact they have to be, the bound alone decides.
A program may use at most 128 MiB of HBM per device.

v0:
```python
import functools
import math

import jax
import jax.numpy as jnp
from jax import lax
from jax.experimental import pallas as pl
from jax.experimental.pallas import tpu as pltpu
from jax.sharding import PartitionSpec as P

MESH = pl.DeviceIdType.MESH
bulk_modulus = 150.0
shear_modulus = 25.0
soft_stretch = 0.05
PAD = 4


def bond_offsets():
    chosen = []
    for step_x in range(0, 4):
        for step_y in range(-3, 4):
            for step_z in range(-3, 4):
                if step_x * step_x + step_y * step_y + step_z * step_z > 9:
                    continue
                if step_x > 0 or (step_x == 0 and (step_y > 0 or (step_y == 0 and step_z > 0))):
                    chosen.append((step_x, step_y, step_z))
    return chosen


def square(offset):
    return sum(step * step for step in offset)


def weighted_volume():
    return 2.0 * sum(math.exp(-square(o) / 9.0) * square(o) for o in bond_offsets())


ORDER = sorted(range(len(bond_offsets())), key=lambda k: (bond_offsets()[k][:2], bond_offsets()[k][2]))


def spread_parts(c, bx, by, bz):
    n, m, mx = -(-bx * c // (bz // 6)), (bx * c + 1) // 2, (3 * c + 1) // 2
    sent = {"z": (n, by, bz), "y+": (m, 8, bz), "y-": (m, 8, bz), "c+": (n, 8, bz), "c-": (n, 8, bz)}
    taken = {}
    for dy in (-1, 0, 1):
        for dz in (-1, 0, 1):
            shape = ((c, 3, by, bz), (1, by, bz), (mx, 8, bz), (1, 8, bz))[2 * abs(dy) + abs(dz)]
            taken[1, dy, dz] = shape
            if dy or dz:
                taken[0, dy, dz] = (None, (n, by, bz), (m, 8, bz), (n, 8, bz))[2 * abs(dy) + abs(dz)]
    return sent, taken


def fold_sent(c, bx, by, bz):
    sent, taken = spread_parts(c, bx, by, bz)
    sent["x"], sent["xz"] = (c, 3, by, bz), (1, by, bz)
    for sign, dy in (("+", 1), ("-", -1)):
        sent["xy" + sign], sent["xc" + sign] = taken[1, dy, 0], taken[1, dy, 1]
    return sent


def scratch_plan(bonds, bx, by, bz):
    rows = by + 2 * PAD
    pairs = len({o[1:] for o in bond_offsets()})
    plan = {"jf": (bonds, bx, by, bz), "ext": (bonds, bx, by, bz), "len": (bonds, bx, by, bz), "mask": (pairs, by, bz)}
    plan["u_in"] = (3, bx, by, bz)
    for name, c in (("u", 3), ("t", 1)):
        sent, taken = spread_parts(c, bx, by, bz)
        n = sent["z"][0]
        plan[name, "field"] = (bx + 3, c, rows, bz)
        plan[name, "shifted"] = plan[name, "sums"] = (7, bx + 3, c, rows, bz)
        plan[name, "main"] = (bx + 3, c, rows, bz)
        plan[name, "pack"] = plan[name, "edges"] = (n + 1, rows, bz)
        for key, shape in sent.items():
            plan[name, "s", key] = shape
        for key, shape in fold_sent(c, bx, by, bz).items():
            plan[name, "fs", key] = shape
        for key, shape in taken.items():
            plan[name, "r", key] = shape
            plan[name, "fr", key] = shape
    return plan


def kernel(sizes, names, u_hbm, intact_hbm, force_out, theta_out, *scratch):
    B = dict(zip(names, scratch))
    intact, send_sem, recv_sem, load_sem = scratch[len(names) :]
    offsets = bond_offsets()
    volume = weighted_volume()
    bx, by, bz = theta_out.shape
    rows = by + 2 * PAD
    per = bz // 6
    axes = ("gx", "gy", "gz")
    index = {a: lax.axis_index(a) for a in axes}
    has = {(a, -1): index[a] > 0 for a in axes}
    has.update({(a, 1): index[a] < sizes[a] - 1 for a in axes})
    own = slice(PAD, PAD + by)
    below, above = slice(0, PAD), slice(PAD + by, rows)
    tiles = [slice(i, i + 8) for i in range(0, rows, 8)]
    jf, ext_s, len_s, mask = B["jf"], B["ext"], B["len"], B["mask"]

    def there(direction):
        found = None
        for a, step in zip(axes, direction):
            if step:
                found = has[a, step] if found is None else found & has[a, step]
        return found

    everyone = [(x, y, z) for x in (-1, 0, 1) for y in (-1, 0, 1) for z in (-1, 0, 1) if x or y or z]
    exists = {d: there(d) for d in everyone}

    def device(direction):
        return {a: index[a] + step for a, step in zip(axes, direction) if step}

    load_u = pltpu.make_async_copy(u_hbm, B["u_in"], load_sem.at[0])
    load_u.start()
    load = pltpu.make_async_copy(intact_hbm, intact, load_sem.at[1])
    load.start()
    for key, ref in B.items():
        if isinstance(key, tuple) and key[1] in ("r", "fr"):
            ref[...] = jnp.zeros(ref.shape, jnp.float32)

    barrier = pltpu.get_barrier_semaphore()
    count = jnp.int32(0)
    for d in everyone:
        count = count + jnp.where(exists[d], 1, 0).astype(jnp.int32)

        @pl.when(exists[d])
        def _(d=d):
            pl.semaphore_signal(barrier, inc=1, device_id=device(d), device_id_type=MESH)

    copies = []

    class Shift:
        def __init__(self, direction, src, dst):
            number = len(copies)
            copies.append(self)
            self.copy = pltpu.make_async_remote_copy(
                src_ref=src, dst_ref=dst, send_sem=send_sem.at[number], recv_sem=recv_sem.at[number],
                device_id=device(direction), device_id_type=MESH,
            )
            self.sends = exists[direction]
            self.takes = exists[tuple(-step for step in direction)]

            @pl.when(self.sends)
            def _():
                self.copy.start()

        def receive(self):
            @pl.when(self.takes)
            def _():
                self.copy.wait_recv()

        def finish(self):
            @pl.when(self.sends)
            def _():
                self.copy.wait_send()

    lane8 = lax.broadcasted_iota(jnp.int32, (8, bz), 1)
    lane = lax.broadcasted_iota(jnp.int32, (by, bz), 1)
    row = lax.broadcasted_iota(jnp.int32, (by, bz), 0)
    edge = (lane < 3) | (lane >= bz - 3)
    first = lax.rem(lane, 6) < 3
    first4 = lax.rem(lax.broadcasted_iota(jnp.int32, (4, bz), 1), 6) < 3
    zeros4 = jnp.zeros((4, bz), jnp.float32)

    def place(x, c, comps):
        group = x % bx * comps + c
        return group // per, 6 * (group % per) + 3

    def half(i):
        return slice(4 * (i % 2), 4 * (i % 2) + 4)

    def roll(value, amount):
        return pltpu.roll(value, amount % bz, 1)

    def planes(comps, low, high):
        return [(x, c) for x in range(low, high) for c in range(comps)]

    signs = (("+", 1), ("-", -1))

    def spread(name, comps, whole):
        field = B[name, "field"]
        z = B[name, "s", "z"]
        n = z.shape[0]
        mx = (3 * comps + 1) // 2
        packed = [None] * n
        for i, (x, c) in enumerate(planes(comps, 0, bx)):
            slot, at = place(x, c, comps)
            moved = roll(jnp.where(edge, field[x, c, own, :], 0.0), at)
            packed[slot] = moved if packed[slot] is None else packed[slot] + moved
            B[name, "s", "y+"][i // 2, half(i), :] = field[x, c, PAD + by - 4 : PAD + by, :]
            B[name, "s", "y-"][i // 2, half(i), :] = field[x, c, PAD : PAD + 4, :]
        for s in range(n):
            z[s] = packed[s]
            B[name, "s", "c+"][s, 0:4, :] = z[s, by - 4 : by, :]
            B[name, "s", "c-"][s, 0:4, :] = z[s, 0:4, :]
            B[name, "s", "c+"][s, 4:8, :] = zeros4
            B[name, "s", "c-"][s, 4:8, :] = zeros4
        return mx, whole

    def spread_send(name, mx, whole):
        sent = {}
        for far in (1, 0):
            for dy in (1, -1, 0):
                for dz in (1, -1, 0):
                    if (far, dy, dz) == (0, 0, 0):
                        continue
                    sign = "+" if dy > 0 else "-"
                    if dy and dz:
                        src = B[name, "s", "c" + sign]
                        src = src.at[0:1] if far else src
                    elif dy:
                        src = B[name, "s", "y" + sign]
                        src = src.at[0:mx] if far else src
                    elif dz:
                        src = B[name, "s", "z"]
                        src = src.at[0:1] if far else src
                    else:
                        src = whole
                    sent[far, dy, dz] = Shift((-far, dy, dz), src, B[name, "r", (far, dy, dz)])
        return sent

    def spread_take(name, comps, sent, far):
        for (f, dy, dz), copy in sent.items():
            if f == far:
                copy.receive()
        field, pack = B[name, "field"], B[name, "pack"]
        n = pack.shape[0] - 1
        R = lambda dy, dz: B[name, "r", (far, dy, dz)]
        for s in range(1 if far else n):
            to = n if far else s
            pack[to, own, :] = jnp.where(first, R(0, 1)[s], R(0, -1)[s])
            pack[to, below, :] = jnp.where(first4, R(1, 1)[s, 0:4, :], R(1, -1)[s, 0:4, :])
            pack[to, above, :] = jnp.where(first4, R(-1, 1)[s, 0:4, :], R(-1, -1)[s, 0:4, :])
        for i, (x, c) in enumerate(planes(comps, 0, 3 if far else bx)):
            to = x + bx if far else x
            if far:
                field[to, c, own, :] = R(0, 0)[c, x]
            field[to, c, below, :] = R(1, 0)[i // 2, half(i), :]
            field[to, c, above, :] = R(-1, 0)[i // 2, half(i), :]
        shifted(name, comps, *((bx, bx + 3) if far else (0, bx)))

    def shifted(name, comps, low, high):
        field, pack, out = B[name, "field"], B[name, "pack"], B[name, "shifted"]
        n = pack.shape[0] - 1
        for x, c in planes(comps, low, high):
            slot, at = place(x, c, comps)
            slot = slot if x < bx else n
            for tile in tiles:
                value = field[x, c, tile, :]
                beyond = roll(pack[slot, tile, :], -at)
                for s in range(-3, 4):
                    if s == 0:
                        moved = value
                    else:
                        fresh = lane8 < s if s > 0 else lane8 >= bz + s
                        moved = roll(jnp.where(fresh, beyond, value), -s)
                    if comps == 3 and c == 2 and s != 0:
                        moved = moved + float(s)
                    out[s + 3, x, c, tile, :] = moved

    def combine(name, comps, low, high):
        sums, main, edges = B[name, "sums"], B[name, "main"], B[name, "edges"]
        n = edges.shape[0] - 1
        total = {}
        for x, c in planes(comps, low, high):
            slot, at = place(x, c, comps)
            slot = slot if x < bx else n
            for i, tile in enumerate(tiles):
                inner = sums[3, x, c, tile, :]
                over = None
                for s in (-3, -2, -1, 1, 2, 3):
                    moved = roll(sums[s + 3, x, c, tile, :], s)
                    wrapped = lane8 < s if s > 0 else lane8 >= bz + s
                    inner = inner + jnp.where(wrapped, 0.0, moved)
                    beyond = jnp.where(wrapped, moved, 0.0)
                    over = beyond if over is None else over + beyond
                main[x, c, tile, :] = inner
                over = roll(over, at)
                total[slot, i] = over if (slot, i) not in total else total[slot, i] + over
        for (slot, i), value in total.items():
            edges[slot, tiles[i], :] = value

    def fold_send(name, comps, far):
        combine(name, comps, *((bx, bx + 3) if far else (0, bx)))
        main, edges = B[name, "main"], B[name, "edges"]
        n = edges.shape[0] - 1
        S = lambda key: B[name, "fs", ("x" + key) if far else key]
        for i, (x, c) in enumerate(planes(comps, 0, 3 if far else bx)):
            at = x + bx if far else x
            if far:
                B[name, "fs", "x"][c, x] = main[at, c, own, :]
            S("y+")[i // 2, half(i), :] = main[at, c, above, :]
            S("y-")[i // 2, half(i), :] = main[at, c, below, :]
        if (comps * (3 if far else bx)) % 2:
            for sign, _ in signs:
                S("y" + sign)[S("y" + sign).shape[0] - 1, 4:8, :] = zeros4
        for s in range(1 if far else n):
            at = n if far else s
            S("z")[s] = edges[at, own, :]
            S("c+")[s, 0:4, :] = edges[at, above, :]
            S("c-")[s, 0:4, :] = edges[at, below, :]
            S("c+")[s, 4:8, :] = zeros4
            S("c-")[s, 4:8, :] = zeros4
        sent = []
        for dy in (1, -1, 0):
            for dz in (1, -1, 0):
                if not (far or dy or dz):
                    continue
                sign = "+" if dy > 0 else "-"
                src = S("c" + sign) if dy and dz else S("y" + sign) if dy else S("z") if dz else B[name, "fs", "x"]
                sent.append(Shift((far, dy, dz), src, B[name, "fr", (far, dy, dz)]))
        return sent

    def fold_take(name, comps, sent, write):
        main = B[name, "main"]
        R = lambda far, dy, dz: B[name, "fr", (far, dy, dz)]
        for copy in sent:
            copy.receive()
        work = B[name, "edges"]
        n = work.shape[0] - 1
        for far in (0, 1):
            for s in range(1 if far else n):
                value = jnp.where(first, R(far, 0, -1)[s], R(far, 0, 1)[s])
                work[s, own, :] = work[s, own, :] + value if far else value
                work[s, PAD : PAD + 4, :] += jnp.where(first4, R(far, 1, -1)[s, 0:4, :], R(far, 1, 1)[s, 0:4, :])
                work[s, PAD + by - 4 : PAD + by, :] += jnp.where(
                    first4, R(far, -1, -1)[s, 0:4, :], R(far, -1, 1)[s, 0:4, :]
                )
        for i, (x, c) in enumerate(planes(comps, 0, bx)):
            upper, lower = R(0, 1, 0)[i // 2, half(i), :], R(0, -1, 0)[i // 2, half(i), :]
            if x < 3:
                upper = upper + R(1, 1, 0)[i // 2, half(i), :]
                lower = lower + R(1, -1, 0)[i // 2, half(i), :]
            main[x, c, PAD : PAD + 4, :] += upper
            main[x, c, PAD + by - 4 : PAD + by, :] += lower
        for x, c in planes(comps, 0, bx):
            slot, at = place(x, c, comps)
            value = main[x, c, own, :] + jnp.where(edge, roll(work[slot, own, :], -at), 0.0)
            if x < 3:
                value = value + R(1, 0, 0)[c, x]
            write(x, c, value)

    u, uz, t, tz = B["u", "field"], B["u", "shifted"], B["t", "field"], B["t", "shifted"]
    acc_t, acc_f = B["t", "sums"], B["u", "sums"]
    load_u.wait()
    for x, c in planes(3, 0, bx):
        u[x, c, own, :] = B["u_in"][c, x]
    mx, whole = spread("u", 3, B["u_in"].at[:, 0:3])
    pl.semaphore_wait(barrier, count)
    sent = spread_send("u", mx, whole)

    pairs = sorted({o[1:] for o in offsets})
    at_y = index["gy"] * by + row
    at_z = index["gz"] * bz + lane
    for i, (ey, ez) in enumerate(pairs):
        inside = (at_y + ey >= 0) & (at_y + ey < sizes["gy"] * by) & (at_z + ez >= 0) & (at_z + ez < sizes["gz"] * bz)
        mask[i] = jnp.where(inside, 1.0, 0.0)

    def clear(acc):
        zeros = jnp.zeros(acc.shape[2:], jnp.float32)

        def body(i, carry):
            for s in range(7):
                acc[s, i] = zeros
            return carry

        lax.fori_loop(0, acc.shape[1], body, 0)

    clear(acc_t)
    load.wait()

    def prepare(x, carry):
        for k in ORDER:
            ex, ey, ez = offsets[k]
            value = intact[k, x].astype(jnp.float32) * mask[pairs.index((ey, ez))]
            if ex:
                value = value * jnp.where((x + ex < bx) | has["gx", 1], 1.0, 0.0)
            jf[k, x] = value
        return carry

    lax.fori_loop(0, bx, prepare, 0)
    clear(acc_f)
    spread_take("u", 3, sent, 0)
    spread_take("u", 3, sent, 1)

    def bond(x, k, mine):
        ex, ey, ez = offsets[k]
        part = slice(PAD + ey, PAD + ey + by)
        other = [uz[ez + 3, x + ex, c, part, :] for c in range(3)]
        if ex:
            other[0] = other[0] + float(ex)
        if ey:
            other[1] = other[1] + float(ey)
        return [other[c] - mine[c] for c in range(3)], part

    def dilate(x, carry):
        mine = [u[x, c, own, :] for c in range(3)]
        total = jnp.zeros((by, bz), jnp.float32)
        for k in ORDER:
            ex, ey, ez = offsets[k]
            d, part = bond(x, k, mine)
            radius = math.sqrt(square(offsets[k]))
            weight = math.exp(-square(offsets[k]) / 9.0)
            long2 = d[0] * d[0] + d[1] * d[1] + d[2] * d[2]
            ext = long2 * lax.rsqrt(long2) - radius
            term = jf[k, x] * (3.0 / volume * weight * radius) * ext
            ext_s[k, x] = ext
            len_s[k, x] = long2
            total = total + term
            acc_t[ez + 3, x + ex, 0, part, :] += term
        acc_t[3, x, 0, own, :] += total
        return carry

    def sweep(work, name, comps):
        lax.fori_loop(0, 3, lambda i, carry: work(bx - 1 - i, carry), 0)
        sent = fold_send(name, comps, 1)
        lax.fori_loop(0, bx - 3, lambda i, carry: work(bx - 4 - i, carry), 0)
        return sent + fold_send(name, comps, 0)

    def soften(part):
        def body(x, carry):
            for k in part:
                radius = math.sqrt(square(offsets[k]))
                weight = math.exp(-square(offsets[k]) / 9.0)
                ext = ext_s[k, x]
                more = 1.0 + (ext * ext) * (1.0 / (radius * soft_stretch) ** 2)
                scale = jf[k, x] * lax.rsqrt(more * more * len_s[k, x])
                a = 3.0 * bulk_modulus / volume * weight * radius
                b = 15.0 * shear_modulus / volume * weight
                len_s[k, x] = scale * (a - b * radius / 3.0)
                ext_s[k, x] = scale * ext * (2.0 * b)
            return carry

        lax.fori_loop(0, bx, body, 0)

    cut = (2 * len(ORDER)) // 3
    sent = sweep(dilate, "t", 1)
    soften(ORDER[:cut])

    def write_theta(x, c, value):
        theta_out[x] = value
        B["t_own"][0, x] = value
        t[x, 0, own, :] = value

    fold_take("t", 1, sent, write_theta)
    mx, whole = spread("t", 1, B["t_own"].at[:, 0:3])
    sent = spread_send("t", mx, whole)
    soften(ORDER[cut:])
    spread_take("t", 1, sent, 0)
    spread_take("t", 1, sent, 1)

    def push(x, carry):
        mine = [u[x, c, own, :] for c in range(3)]
        here = t[x, 0, own, :]
        total = [jnp.zeros((by, bz), jnp.float32) for c in range(3)]
        for k in ORDER:
            ex, ey, ez = offsets[k]
            d, part = bond(x, k, mine)
            scalar = len_s[k, x] * (here + tz[ez + 3, x + ex, 0, part, :]) + ext_s[k, x]
            for c in range(3):
                pushed = scalar * d[c]
                total[c] = total[c] + pushed
                acc_f[ez + 3, x + ex, c, part, :] -= pushed
        for c in range(3):
            acc_f[3, x, c, own, :] += total[c]
        return carry

    sent = sweep(push, "u", 3)

    def write_force(x, c, value):
        force_out[c, x] = value

    fold_take("u", 3, sent, write_force)
    for copy in copies:
        copy.finish()


def shards(sizes, displacement, bond_intact):
    plan = scratch_plan(bond_intact.shape[0], *displacement.shape[1:])
    plan["t_own"] = (1,) + displacement.shape[1:]
    scratch = [pltpu.VMEM(shape, jnp.float32) for shape in plan.values()]
    scratch += [
        pltpu.VMEM(bond_intact.shape, jnp.int32),
        pltpu.SemaphoreType.DMA((68,)),
        pltpu.SemaphoreType.DMA((68,)),
        pltpu.SemaphoreType.DMA((2,)),
    ]
    vmem, anywhere = pl.BlockSpec(memory_space=pltpu.VMEM), pl.BlockSpec(memory_space=pl.ANY)
    return pl.pallas_call(
        functools.partial(kernel, sizes, tuple(plan)),
        out_shape=(
            jax.ShapeDtypeStruct(displacement.shape, jnp.float32),
            jax.ShapeDtypeStruct(displacement.shape[1:], jnp.float32),
        ),
        in_specs=[anywhere, anywhere],
        out_specs=(vmem, vmem),
        scratch_shapes=scratch,
        compiler_params=pltpu.CompilerParams(collective_id=0, has_side_effects=True, vmem_limit_bytes=56000000),
    )(displacement, bond_intact)


def solution(mesh):
    sizes = {a: mesh.shape[a] for a in ("gx", "gy", "gz")}
    return jax.shard_map(
        functools.partial(shards, sizes),
        mesh=mesh,
        in_specs=(P(None, "gx", "gy", "gz"), P(None, "gx", "gy", "gz")),
        out_specs=(P(None, "gx", "gy", "gz"), P("gx", "gy", "gz")),
        check_vma=False,
    )
```

profile of v0, /device:TPU:1, one launch (start us, length us, event | category | flops | bytes accessed | tf_op | source)
XLA Modules:
  0.0 32.0 jit_solution(16167824370692166222)
XLA Ops:
  0.6 0.0 copy-start
  0.6 0.9 %copy-done = f32[3,8,8,128]{3,2,1,0:T(8,128)S(1)} copy-done((f32[3,8,8,128]{3,2,1,0:T(8,128)S(1)}, f32[3,8,8,128]{3,2,1,0:T(8,128)}, u32[]{:S(2)}) %copy-start) | copy-done | bytes 98328
  1.5 29.2 %shard_map.41 = (f32[3,8,8,128]{3,2,1,0:T(8,128)S(1)}, f32[8,8,128]{2,1,0:T(8,128)S(1)}) custom-call(f32[3,8,8,128]{3,2,1,0:T(8,128)S(1)} %copy-done, s32[61,8,8,128]{3,2,1,0:T(8,128)} %intact_hbm.1), custom_call_target="tpu_custom_call" | custom-call | tf_op jit(solution)/shard_map/pallas_call | solution.py:490
  30.7 0.6 %copy.6 = f32[3,8,8,128]{3,2,1,0:T(8,128)} copy(f32[3,8,8,128]{3,2,1,0:T(8,128)S(1)} %get-tuple-element.4) | data formatting | bytes 196608
  31.3 0.6 %copy.7 = f32[8,8,128]{2,1,0:T(8,128)} copy(f32[8,8,128]{2,1,0:T(8,128)S(1)} %get-tuple-element.5) | data formatting | bytes 65536
Async XLA Ops:
  0.6 0.9 %copy-start = (f32[3,8,8,128]{3,2,1,0:T(8,128)S(1)}, f32[3,8,8,128]{3,2,1,0:T(8,128)}, u32[]{:S(2)}) copy-start(f32[3,8,8,128]{3,2,1,0:T(8,128)} %u_hbm.1) | copy-start | bytes 294916
where the time goes:
time: 32.5 us; the launch traced here: 32 us
  Pallas kernels  29.2 us (90%)
  local copies, waits for them, and re-layouts  2.14 us (7%)
  between operations  0.65 us (2%)
    pallas_call x1, Pallas kernels, shards(): pl.pallas_call(functools.partial(kernel, sizes, tuple(plan)), out_shape=(...  29.2 us
    unnamed x4, local copies, waits for them, and re-layouts  2.14 us

commit v1 on v0

v1 whole, which is shorter than its diff:
```python
import functools
import math

import jax
import jax.numpy as jnp
from jax import lax
from jax.experimental import pallas as pl
from jax.experimental.pallas import tpu as pltpu
from jax.sharding import PartitionSpec as P

MESH = pl.DeviceIdType.MESH
bulk_modulus = 150.0
shear_modulus = 25.0
soft_stretch = 0.05
AXES = ("gx", "gy", "gz")
H = 3
PAD = 4
GROUP = 8


def bond_offsets():
    chosen = []
    for step_x in range(0, 4):
        for step_y in range(-3, 4):
            for step_z in range(-3, 4):
                if step_x * step_x + step_y * step_y + step_z * step_z > 9:
                    continue
                if step_x > 0 or (step_x == 0 and (step_y > 0 or (step_y == 0 and step_z > 0))):
                    chosen.append((step_x, step_y, step_z))
    return chosen


OFFSETS = bond_offsets()
NUMBER = {o: k for k, o in enumerate(OFFSETS)}
ORDER = sorted(range(len(OFFSETS)), key=lambda k: (OFFSETS[k][:2], OFFSETS[k][2]))


def square(offset):
    return sum(step * step for step in offset)


VOLUME = 2.0 * sum(math.exp(-square(o) / 9.0) * square(o) for o in OFFSETS)


def minus(offset):
    return tuple(-step for step in offset)


def bond_of(step):
    return (NUMBER[step], True) if step in NUMBER else (NUMBER[minus(step)], False)


def radius_of(k):
    return math.sqrt(square(OFFSETS[k]))


def terms(k):
    weight, radius = math.exp(-square(OFFSETS[k]) / 9.0), radius_of(k)
    c = 3.0 / VOLUME * weight * radius
    a = 3.0 * bulk_modulus / VOLUME * weight * radius
    b = 15.0 * shear_modulus / VOLUME * weight
    return c, (a - b * radius / 3.0) / c, 2.0 * b / c


STEPS = [s for o in OFFSETS for s in (o, minus(o))]
PAIRS = sorted({s[1:] for s in STEPS})
FIRST = {}
LAST = {}
for _k, _o in enumerate(OFFSETS):
    FIRST.setdefault(_o[0], _k)
    LAST[_o[0]] = _k + 1
RUNS = {}
for _k, _o in enumerate(OFFSETS):
    if _o[1]:
        RUNS.setdefault(_o[:2], []).append(_k)
RUNS = {g: (ks[0], ks[-1] + 1) for g, ks in RUNS.items()}

SLOTS = sorted(
    {(o[0], o[1], abs(o[2])) for o in OFFSETS if o[2]},
    key=lambda s: ((0 if s[1] > 0 else 1 if s[1] < 0 else 2), s[0] if s[1] else -s[0], s),
)
SLOT = {s: i for i, s in enumerate(SLOTS)}
STRIP = sorted({(s[0], s[1], abs(s[2])) for s in STEPS if s[2]})
MOVES = sorted({(s[0], s[2]) for s in STRIP})


def span(test):
    found = [i for i, s in enumerate(SLOTS) if test(s)]
    assert found == list(range(found[0], found[-1] + 1))
    return slice(found[0], found[-1] + 1)


def side(step, size, at):
    return slice(at - H, at) if step < 0 else slice(at + size, at + size + H) if step > 0 else slice(at, at + size)


def edge_of(step, size, at):
    return slice(at, at + H) if step < 0 else slice(at + size - H, at + size) if step > 0 else slice(at, at + size)


def evaluations(bx, by):
    x_list, y_list = [], []
    for x in range(bx):
        x_list += [("x", x, s) for s in sorted(STEPS, key=lambda s: (s[1], s[2])) if not 0 <= x + s[0] < bx]
    for r in range(by):
        y_list += [("y", r, s) for s in sorted(STEPS, key=lambda s: (s[0], s[2])) if not 0 <= r + s[1] < by]
    return x_list, y_list, [("z", 0, s) for s in STRIP]


def scratch_plan(bonds, bx, by, bz):
    rows, planes, f, i = by + 2 * PAD, 2 * bx, jnp.float32, jnp.int32
    halo = sum(len(part) for part in evaluations(bx, by))
    plan = {"jf": (f, (bonds, bx, by, bz)), "ext": (f, (bonds, bx, by, bz)), "len": (f, (bonds, bx, by, bz))}
    plan["d"] = (f, (bonds, bx, 3, by, bz))
    plan["hj"] = plan["hext"] = plan["hlen"] = (f, (halo, by, bz))
    plan["hd"] = (f, (halo, 3, by, bz))
    plan["mask"] = (f, (len(PAIRS), by, bz))
    plan["lanes"] = (f, (7, by, bz))
    plan["ix"] = (i, (bonds, H, rows, bz))
    plan["iy"] = (i, (bonds, bx, by, bz))
    plan["own_slots"] = (f, (len(SLOTS), by, bz))
    plan["slots"] = (f, (2, 2, len(SLOTS), rows, bz))
    for name, c in (("u", 3), ("t", 1)):
        plan[name, "field"] = (f, (c, planes, rows, bz))
        plan[name, "main"] = (f, (7, c, bx + H, rows, bz))
        plan[name, "sums"] = (f, (7, bx + H, c, rows, bz))
        plan[name, "base"] = (f, (c, bx, by, bz))
        plan[name, "x"] = (f, (7, c, 2 * H, rows, bz))
        plan[name, "y"] = (f, (7, c, 2 * H, planes, bz))
        plan[name, "in"] = (f, (c, by, bz))
        plan[name, "z"] = (f, (2, 3, c, rows, bz))
        plan[name, "q"] = (f, (len(MOVES), c, rows, bz))
    return plan


def kernel(sizes, names, u_hbm, intact_hbm, force_out, theta_out, *scratch):
    B = dict(zip(names, scratch))
    intact, send_sem, recv_sem, load_sem = scratch[len(names) :]
    bx, by, bz = theta_out.shape
    rows, planes = by + 2 * PAD, 2 * bx
    assert bx == by and planes * GROUP == bz and GROUP >= 2 * H + 2
    x_list, y_list, z_list = evaluations(bx, by)
    everything = x_list + y_list + z_list
    place = {e: i for i, e in enumerate(everything)}
    index = {a: lax.axis_index(a) for a in AXES}
    has = {(a, -1): index[a] > 0 for a in AXES}
    has.update({(a, 1): index[a] < sizes[a] - 1 for a in AXES})
    own = slice(PAD, PAD + by)

    def there(direction):
        found = None
        for a, step in zip(AXES, direction):
            if step:
                found = has[a, step] if found is None else found & has[a, step]
        return found

    everyone = [(x, y, z) for x in (-1, 0, 1) for y in (-1, 0, 1) for z in (-1, 0, 1) if x or y or z]
    exists = {d: there(d) for d in everyone}

    def device(direction):
        return {a: index[a] + step for a, step in zip(AXES, direction) if step}

    u = B["u", "field"]
    load_u = pltpu.make_async_copy(u_hbm, u.at[:, H : H + bx, own, :], load_sem.at[0])
    load_u.start()
    load = pltpu.make_async_copy(intact_hbm, intact, load_sem.at[1])
    load.start()

    barrier = pltpu.get_barrier_semaphore()
    count = jnp.int32(0)
    for d in everyone:
        count = count + jnp.where(exists[d], 1, 0).astype(jnp.int32)

        @pl.when(exists[d])
        def _(d=d):
            pl.semaphore_signal(barrier, inc=1, device_id=device(d), device_id_type=MESH)

    copies = []

    class Shift:
        def __init__(self, direction, src, dst):
            number = len(copies)
            copies.append(self)
            self.direction = direction
            self.copy = pltpu.make_async_remote_copy(
                src_ref=src, dst_ref=dst, send_sem=send_sem.at[number], recv_sem=recv_sem.at[number],
                device_id=device(direction), device_id_type=MESH,
            )
            self.sends = exists[direction]
            self.takes = exists[minus(direction)]

            @pl.when(self.sends)
            def _():
                self.copy.start()

        def receive(self):
            @pl.when(self.takes)
            def _():
                self.copy.wait_recv()

        def finish(self):
            @pl.when(self.sends)
            def _():
                self.copy.wait_send()

    def nothing(view):
        view[...] = jnp.zeros(view.shape, view.dtype)

    def landing(name, d):
        if d[2]:
            return B[name, "z"].at[(d[2] + 1) // 2, d[0] + 1, :, side(d[1], by, PAD), :]
        return B[name, "field"].at[:, side(d[0], bx, H), side(d[1], by, PAD), :]

    SENT = (slice(0, by), slice(by - 2, by), slice(0, 2))
    LAND = (slice(PAD, PAD + by), slice(PAD - 2, PAD), slice(PAD + by, PAD + by + 2))
    up, down = span(lambda s: s[1] > 0), span(lambda s: s[1] < 0)
    x_all, x_up = span(lambda s: s[0] > 0), span(lambda s: s[0] > 0 and s[1] > 0)
    slot_moves = []
    for dz in (-1, 1):
        for dx, parts in ((0, (slice(0, len(SLOTS)), up, down)), (1, (x_all, x_up, down))):
            for way, dy in enumerate((0, 1, -1)):
                slot_moves.append(((dx, dy, dz), parts[way], way))

    def slot_landing(d, part, way):
        return B["slots"].at[(1 - d[2]) // 2, d[0], part, LAND[way], :]

    for d in everyone:

        @pl.when(jnp.logical_not(exists[d]))
        def _(d=d):
            for name in ("u", "t"):
                nothing(landing(name, d))
            for e, part, way in slot_moves:
                if minus(e) == d:
                    nothing(slot_landing(e, part, way))
            if d == (-1, 0, 0):
                nothing(B["ix"])
            for (ex, ey), (k0, k1) in RUNS.items():
                back = -1 if ey > 0 else 1
                at = slice(by - ey, by) if ey > 0 else slice(0, -ey)
                if d == (0, back, 0):
                    nothing(B["iy"].at[k0:k1, ex:, at, :])
                if ex and d == (-1, back, 0):
                    nothing(B["iy"].at[k0:k1, 0:ex, at, :])

    lane = lax.broadcasted_iota(jnp.int32, (by, bz), 1)
    row = lax.broadcasted_iota(jnp.int32, (by, bz), 0)
    spot = lax.rem(lane, GROUP)
    high = spot >= GROUP // 2
    edge = (lane < H) | (lane >= bz - H)
    inner = (lane >= H * GROUP) & (lane < (H + bx) * GROUP)
    zero = jnp.zeros((by, bz), jnp.float32)

    def number(condition):
        return jnp.where(condition, 1.0, 0.0)

    def roll(value, amount):
        return pltpu.roll(value, amount % bz, 1) if amount % bz else value

    def to_strip(total):
        return jnp.where(high, roll(total, GROUP), total)

    def pack(tiles):
        total = zero
        for x, tile in enumerate(tiles):
            total = total + roll(jnp.where(edge, tile, 0.0), GROUP * (x + H))
        return to_strip(total)

    def unpack(strip):
        strip = jnp.where(high, roll(strip, -GROUP), strip)
        return [jnp.where(edge, roll(strip, -GROUP * (x + H)), 0.0) for x in range(bx)]

    def flat(ref, *at):
        return ref.reshape(*ref.shape[:-3], ref.shape[-3] * ref.shape[-2], bz)

    u_flat, t_flat, intact_flat = flat(u), flat(B["t", "field"]), flat(intact)
    iy_flat = flat(B["iy"])

    def clear(ref, depth):
        zeros = jnp.zeros(ref.shape[2:], jnp.float32)

        def body(i, carry):
            for s in range(depth):
                ref[s, i] = zeros
            return carry

        lax.fori_loop(0, ref.shape[1], body, 0)

    for name in ("u", "t"):
        main, beside = B[name, "main"], B[name, "x"]
        for c in range(main.shape[1]):
            for s in range(7):

                def blank(i, carry, s=s, c=c, main=main):
                    main[s, c, i] = jnp.zeros((rows, bz), jnp.float32)
                    return carry

                lax.fori_loop(0, bx + H, blank, 0)

                def blank_x(i, carry, s=s, c=c, beside=beside):
                    beside[s, c, i] = jnp.zeros((rows, bz), jnp.float32)
                    return carry

                lax.fori_loop(0, 2 * H, blank_x, 0)
    clear(B["t", "sums"], 7)
    clear(B["u", "sums"], 7)

    for i, (ey, ez) in enumerate(PAIRS):
        B["mask"][i] = number((row + ey >= 0) & (row + ey < by) & (lane + ez >= 0) & (lane + ez < bz))
    for ez in range(-H, H + 1):
        B["lanes"][ez + H] = number((lane + ez >= 0) & (lane + ez < bz))

    def mask(ey, ez):
        return B["mask"][PAIRS.index((ey, ez))]

    def shift_main(name):
        field, out = B[name, "field"], B[name, "main"]
        for c in range(field.shape[0]):

            def body(x, carry, c=c):
                value = field[c, x + H, own, :]
                for ez in range(-H, H + 1):
                    out[ez + H, c, x, own, :] = roll(value, -ez)
                return carry

            lax.fori_loop(0, bx, body, 0)

    load_u.wait()
    for c in range(3):
        B["u", "in"][c] = pack([u[c, x + H, own, :] for x in range(bx)])
    load.wait()

    beyond_x = number(has["gx", 1])
    z_up, z_down = number(has["gz", 1]), number(has["gz", -1])

    def slots_body(x, totals):
        new = []
        crossing = jnp.where(has["gx", 1], 1.0, 0.0)
        for (ex, ey, az), total in zip(SLOTS, totals):
            value = jnp.where(lane >= bz - az, intact[NUMBER[ex, ey, az], x].astype(jnp.float32) * z_up, 0.0)
            if (ex, ey, -az) in NUMBER:
                other = intact[NUMBER[ex, ey, -az], x].astype(jnp.float32) * z_down
                value = jnp.where(lane < az, other, value)
            if ex:
                value = value * jnp.where(x + ex < bx, 1.0, crossing)
            new.append(total + pltpu.roll(value, GROUP * (x + H), 1))
        return tuple(new)

    totals = lax.fori_loop(0, bx, slots_body, tuple(zero for _ in SLOTS))
    y_inside = {}
    for ey in range(-H, H + 1):
        inside = (row + ey >= 0) & (row + ey < by)
        y_inside[ey] = jnp.where(inside, 1.0, number(has["gy", 1 if ey > 0 else -1])) if ey else None
    for (ex, ey, az), total in zip(SLOTS, totals):
        value = to_strip(total) * terms(NUMBER[ex, ey, az])[0]
        B["own_slots"][SLOT[ex, ey, az]] = value * y_inside[ey] if ey else value

    pl.semaphore_wait(barrier, count)

    def spread(name, far=False):
        field, strip = B[name, "field"], B[name, "in"]
        sent = []
        for d in sorted(everyone, key=lambda d: -sum(map(abs, d))):
            if d[2]:
                src = strip.at[:, edge_of(d[1], by, 0), :]
            else:
                src = field.at[:, edge_of(d[0], bx, H), edge_of(d[1], by, PAD), :]
            sent.append(Shift(d, src, landing(name, minus(d))))
        return sent

    sent_u = spread("u")
    sent_i = []
    for (ex, ey), (k0, k1) in RUNS.items():
        toward = 1 if ey > 0 else -1
        at = slice(by - ey, by) if ey > 0 else slice(0, -ey)
        if ex:
            sent_i.append(
                Shift((1, toward, 0), intact.at[k0:k1, bx - ex :, at, :], B["iy"].at[k0:k1, 0:ex, at, :])
            )
    for e, part, way in reversed(slot_moves):
        sent_i.append(Shift(e, B["own_slots"].at[part, SENT[way], :], slot_landing(e, part, way)))
    for (ex, ey), (k0, k1) in RUNS.items():
        toward = 1 if ey > 0 else -1
        at = slice(by - ey, by) if ey > 0 else slice(0, -ey)
        sent_i.append(
            Shift((0, toward, 0), intact.at[k0:k1, 0 : bx - ex, at, :], B["iy"].at[k0:k1, ex:, at, :])
        )
    for ex in range(1, H + 1):
        k0, k1 = FIRST[ex], LAST[ex]
        sent_i.append(Shift((1, 0, 0), intact.at[k0:k1, bx - ex :, :, :], B["ix"].at[k0:k1, 0:ex, own, :]))

    shift_main("u")

    def prepare(x, carry):
        for k in ORDER:
            ex, ey, ez = OFFSETS[k]
            factor = jnp.where(x + ex < bx, terms(k)[0], 0.0) if ex else terms(k)[0]
            B["jf"][k, x] = intact[k, x].astype(jnp.float32) * mask(ey, ez) * factor
        return carry

    lax.fori_loop(0, bx, prepare, 0)

    y_planes = {}
    for ex in range(H + 1):
        y_planes[ex] = jnp.where(row + ex < bx, 1.0, beyond_x)

    def own_flags(e):
        kind, at, step = e
        k, mine = bond_of(step)
        if kind == "x":
            return intact[k, at].astype(jnp.float32) * mask(*step[1:]) * (terms(k)[0] * beyond_x)
        value = intact_flat[k, pl.ds(at, bx, stride=by), :].astype(jnp.float32) * B["lanes"][step[2] + H]
        return value * (y_planes[step[0]] * (terms(k)[0] * number(has["gy", 1 if step[1] > 0 else -1])))

    for e in x_list + y_list:
        if bond_of(e[2])[1]:
            B["hj"][place[e]] = own_flags(e)

    def length(d, k):
        long2 = d[0] * d[0] + d[1] * d[1] + d[2] * d[2]
        return long2, long2 * lax.rsqrt(long2) - radius_of(k)

    acc_t, acc_f = B["t", "sums"], B["u", "sums"]
    uz, tz = B["u", "main"], B["t", "main"]

    def dilate(x, carry):
        mine = [u[c, x + H, own, :] for c in range(3)]
        near = [{v: mine[c] - float(v) if v else mine[c] for v in range(-H, H + 1)} for c in range(3)]
        total = zero
        for k in ORDER:
            ex, ey, ez = OFFSETS[k]
            part = slice(PAD + ey, PAD + ey + by)
            d = [uz[ez + H, c, x + ex, part, :] - near[c][OFFSETS[k][c]] for c in range(3)]
            long2, ext = length(d, k)
            term = B["jf"][k, x] * ext
            for c in range(3):
                B["d"][k, x, c] = d[c]
            B["ext"][k, x] = ext
            B["len"][k, x] = long2
            total = total + term
            acc_t[ez + H, x + ex, 0, part, :] += term
        B["t", "base"][0, x] = total
        return carry

    lax.fori_loop(0, bx, dilate, 0)

    def gather(name):
        sums, base = B[name, "sums"], B[name, "base"]
        for c in range(base.shape[0]):

            def body(x, carry, c=c):
                value = base[c, x] + sums[H, x, c, own, :]
                for ez in (-3, -2, -1, 1, 2, 3):
                    value = value + roll(sums[ez + H, x, c, own, :], ez) * B["lanes"][H - ez]
                base[c, x] = value
                return carry

            lax.fori_loop(0, bx, body, 0)

    gather("t")

    def soften_one(j, ext, long2, k):
        _, p, q = terms(k)
        more = 1.0 + (ext * ext) * (1.0 / (radius_of(k) * soft_stretch) ** 2)
        scale = j * lax.rsqrt(more * more * long2)
        return scale * p, scale * ext * q

    def soften(x, carry):
        for k in ORDER:
            B["len"][k, x], B["ext"][k, x] = soften_one(B["jf"][k, x], B["ext"][k, x], B["len"][k, x], k)
        return carry

    lax.fori_loop(0, bx, soften, 0)

    def beside(name):
        field, z = B[name, "field"], B[name, "z"]
        field_flat = u_flat if name == "u" else t_flat
        comps = field.shape[0]
        for c in range(comps):
            for i in range(2 * H):
                plane = i if i < H else i + bx
                value = field[c, plane, own, :]
                for ez in range(-H, H + 1):
                    B[name, "x"][ez + H, c, i, own, :] = roll(value, -ez)
                at = PAD - H + i if i < H else PAD + by + i - H
                for half in range(2):
                    value = field_flat[c, pl.ds(half * bx * rows + at, bx, stride=rows), :]
                    for ez in range(-H, H + 1):
                        B[name, "y"][ez + H, c, i, half * bx : half * bx + bx, :] = roll(value, -ez)
            for tile in (slice(0, by), slice(by, rows)):
                near, left, right = [jnp.where(high, z[0, i, c, tile, :], z[1, i, c, tile, :]) for i in (1, 0, 2)]
                far = roll(jnp.where(lane < bz // 2 - GROUP, right, left), bx * GROUP)
                value = jnp.where(inner, near, far)
                for i, (ex, az) in enumerate(MOVES):
                    over = roll(value, GROUP - GROUP * ex - az)
                    under = roll(value, -GROUP - GROUP * ex + az)
                    B[name, "q"][i, c, tile, :] = jnp.where(high, over, under)

    for copy in sent_u:
        copy.receive()
    beside("u")

    strip_sign = jnp.where(high, 1.0, -1.0)

    def other(name, e, c):
        kind, at, (ex, ey, ez) = e
        if kind == "x":
            i = at + ex + H if at + ex < 0 else at + ex - bx + H
            return B[name, "x"][ez + H, c, i, PAD + ey : PAD + ey + by, :]
        if kind == "y":
            i = at + ey + H if at + ey < 0 else at + ey - by + H
            return B[name, "y"][ez + H, c, i, H + ex : H + ex + bx, :]
        return B[name, "q"][MOVES.index((ex, ez)), c, PAD + ey : PAD + ey + by, :]

    def inside(name, kind, at, c):
        if kind == "x":
            return B[name, "field"][c, at + H, own, :]
        if kind == "y":
            flat_field = u_flat if name == "u" else t_flat
            return flat_field[c, pl.ds(H * rows + PAD + at, bx, stride=rows), :]
        return B[name, "in"][c]

    def bond(e):
        return NUMBER[e[2]] if e[0] == "z" and e[2] in NUMBER else bond_of(e[2])[0]

    def stretch(part, total):
        near, was = {}, None
        for e in part:
            kind, at, step = e
            if (kind, at) != was:
                was, near = (kind, at), {}
            i, k = place[e], bond(e)
            d = []
            for c in range(3):
                if (c, step[c]) not in near:
                    if (c, None) not in near:
                        near[c, None] = inside("u", kind, at, c)
                    start = near[c, None]
                    if step[c]:
                        move = strip_sign * float(step[c]) if kind == "z" and c == 2 else float(step[c])
                        start = start - move
                    near[c, step[c]] = start
                d.append(other("u", e, c) - near[c, step[c]])
            long2, ext = length(d, k)
            for c in range(3):
                B["hd"][i, c] = d[c]
            B["hext"][i] = ext
            B["hlen"][i] = long2
            term = B["hj"][i] * ext
            total[kind, at] = total[kind, at] + term if (kind, at) in total else term

    def from_slots(ex, ey, az):
        got, s = B["slots"], SLOT[ex, ey, az]
        part = slice(PAD - ey, PAD - ey + by)
        value = jnp.where(high, got[0, 0, s, part, :], got[1, 0, s, part, :])
        if ex:
            far = jnp.where(high, got[0, 1, s, part, :], got[1, 1, s, part, :])
            value = jnp.where(inner, value, roll(far, bx * GROUP))
        over = roll(value, GROUP + GROUP * ex - az)
        under = roll(value, -GROUP + GROUP * ex + az)
        return jnp.where(spot >= GROUP - az, over, jnp.where(spot < az, under, 0.0))

    def taken_flags(e):
        kind, at, step = e
        ex, ey, ez = minus(step)
        k = NUMBER[ex, ey, ez]
        if kind == "x":
            value = B["ix"][k, at, PAD - ey : PAD - ey + by, :].astype(jnp.float32)
            return roll(value, ez) * (mask(*step[1:]) * terms(k)[0])
        from_row = at - ey + by if ey > 0 else at - ey - by
        value = iy_flat[k, pl.ds(from_row, bx, stride=by), :].astype(jnp.float32)
        return roll(value, ez) * (B["lanes"][step[2] + H] * terms(k)[0])

    sums_t = {}
    stretch([e for e in x_list + y_list if bond_of(e[2])[1]], sums_t)
    for copy in sent_i:
        copy.receive()
    for e in x_list + y_list:
        if not bond_of(e[2])[1]:
            B["hj"][place[e]] = taken_flags(e)
    for e in z_list:
        ex, ey, az = e[2]
        value = B["own_slots"][SLOT[e[2]]] if e[2] in SLOT else None
        if (-ex, -ey, az) in SLOT:
            more = from_slots(-ex, -ey, az)
            value = more if value is None else value + more
        B["hj"][place[e]] = value
    stretch([e for e in x_list + y_list if not bond_of(e[2])[1]], sums_t)
    stretch(z_list, sums_t)

    def finish(name, c, total, write):
        base = B[name, "base"]
        base_flat = flat(base)
        for r in range(by):
            if ("y", r) in total:
                base_flat[c, pl.ds(r, bx, stride=by), :] += total["y", r]
        for x, strip in enumerate(unpack(total["z", 0])):
            value = base[c, x] + strip
            if ("x", x) in total:
                value = value + total["x", x]
            write(x, value)

    t = B["t", "field"]
    own_theta = []

    def write_theta(x, value):
        theta_out[x] = value
        t[0, x + H, own, :] = value
        own_theta.append(value)

    finish("t", 0, sums_t, write_theta)
    B["t", "in"][0] = pack(own_theta)
    sent_t = spread("t")

    shift_main("t")

    def push(x, carry):
        here = t[0, x + H, own, :]
        total = [zero, zero, zero]
        for k in ORDER:
            ex, ey, ez = OFFSETS[k]
            part = slice(PAD + ey, PAD + ey + by)
            scalar = B["len"][k, x] * (here + tz[ez + H, 0, x + ex, part, :]) + B["ext"][k, x]
            for c in range(3):
                pushed = scalar * B["d"][k, x, c]
                total[c] = total[c] + pushed
                acc_f[ez + H, x + ex, c, part, :] -= pushed
        for c in range(3):
            B["u", "base"][c, x] = total[c]
        return carry

    lax.fori_loop(0, bx, push, 0)
    gather("u")
    for e in everything:
        i = place[e]
        B["hlen"][i], B["hext"][i] = soften_one(B["hj"][i], B["hext"][i], B["hlen"][i], bond(e))

    for copy in sent_t:
        copy.receive()
    beside("t")
    sums_f = [{}, {}, {}]
    for e in everything:
        kind, at, _ = e
        i = place[e]
        scalar = B["hlen"][i] * (inside("t", kind, at, 0) + other("t", e, 0)) + B["hext"][i]
        for c in range(3):
            pushed = scalar * B["hd"][i, c]
            total = sums_f[c]
            total[kind, at] = total[kind, at] + pushed if (kind, at) in total else pushed

    for c in range(3):

        def write_force(x, value, c=c):
            force_out[c, x] = value

        finish("u", c, sums_f[c], write_force)
    for copy in copies:
        copy.finish()


def shards(sizes, displacement, bond_intact):
    plan = scratch_plan(bond_intact.shape[0], *displacement.shape[1:])
    scratch = [pltpu.VMEM(shape, dtype) for dtype, shape in plan.values()]
    scratch += [
        pltpu.VMEM(bond_intact.shape, jnp.int32),
        pltpu.SemaphoreType.DMA((96,)),
        pltpu.SemaphoreType.DMA((96,)),
        pltpu.SemaphoreType.DMA((2,)),
    ]
    vmem, anywhere = pl.BlockSpec(memory_space=pltpu.VMEM), pl.BlockSpec(memory_space=pl.ANY)
    return pl.pallas_call(
        functools.partial(kernel, sizes, tuple(plan)),
        out_shape=(
            jax.ShapeDtypeStruct(displacement.shape, jnp.float32),
            jax.ShapeDtypeStruct(displacement.shape[1:], jnp.float32),
        ),
        in_specs=[anywhere, anywhere],
        out_specs=(vmem, vmem),
        scratch_shapes=scratch,
        compiler_params=pltpu.CompilerParams(collective_id=0, has_side_effects=True, vmem_limit_bytes=62000000),
    )(displacement, bond_intact)


def solution(mesh):
    sizes = {a: mesh.shape[a] for a in AXES}
    return jax.shard_map(
        functools.partial(shards, sizes),
        mesh=mesh,
        in_specs=(P(None, "gx", "gy", "gz"), P(None, "gx", "gy", "gz")),
        out_specs=(P(None, "gx", "gy", "gz"), P("gx", "gy", "gz")),
        check_vma=False,
    )
```

time: 32.5 us -> 25.1 us (0.77)
  Pallas kernels: 29.2 us -> 21.3 us
  local copies, waits for them, and re-layouts: 2.14 us -> 2.91 us
    pallas_call x1, Pallas kernels: 29.2 us -> 21.3 us  [shards(): pl.pallas_call(functools.partial(kernel, sizes, tuple(plan)), out_shape=(...]
    unnamed x4 -> x2, local copies, waits for them, and re-layouts: 2.14 us -> 2.91 us
where the time goes in v1:
time: 25.1 us; the launch traced here: 24.8 us
  Pallas kernels  21.3 us (85%)
  local copies, waits for them, and re-layouts  2.91 us (12%)
  between operations  0.64 us (3%)
    pallas_call x1, Pallas kernels, shards(): pl.pallas_call(functools.partial(kernel, sizes, tuple(plan)), out_shape=(...  21.3 us
    unnamed x2, local copies, waits for them, and re-layouts  2.91 us

profile of v1, /device:TPU:1, one launch (start us, length us, event | category | flops | bytes accessed | tf_op | source)
XLA Modules:
  0.0 24.8 jit_solution(625954286799193921)
XLA Ops:
  0.6 21.3 %shard_map.41 = (f32[3,8,8,128]{3,2,1,0:T(8,128)}, f32[8,8,128]{2,1,0:T(8,128)}) custom-call(f32[3,8,8,128]{3,2,1,0:T(8,128)} %u_hbm.1, s32[61,8,8,128]{3,2,1,0:T(8,128)} %intact_hbm.1), custom_call_target="tpu_custom_call" | custom-call | tf_op jit(solution)/shard_map/pallas_call | solution.py:671
  21.9 1.5 %copy.6 = f32[3,8,8,128]{3,2,1,0:T(8,128)} copy(f32[3,8,8,128]{3,2,1,0:T(8,128)} %get-tuple-element.4) | data formatting | bytes 196608
  23.5 1.4 %copy.7 = f32[8,8,128]{2,1,0:T(8,128)} copy(f32[8,8,128]{2,1,0:T(8,128)} %get-tuple-element.5) | data formatting | bytes 65536

commit v2 on v1

--- a/solution.py
+++ b/solution.py
@@ -224,6 +224,128 @@
     def slot_landing(d, part, way):
         return B["slots"].at[(1 - d[2]) // 2, d[0], part, LAND[way], :]
 
+    lane = lax.broadcasted_iota(jnp.int32, (by, bz), 1)
+    row = lax.broadcasted_iota(jnp.int32, (by, bz), 0)
+    spot = lax.rem(lane, GROUP)
+    high = spot >= GROUP // 2
+    edge = (lane < H) | (lane >= bz - H)
+    inner = (lane >= H * GROUP) & (lane < (H + bx) * GROUP)
+    zero = jnp.zeros((by, bz), jnp.float32)
+
+    def number(condition):
+        return jnp.where(condition, 1.0, 0.0)
+
+    def roll(value, amount):
+        return pltpu.roll(value, amount % bz, 1) if amount % bz else value
+
+    def to_strip(total):
+        return jnp.where(high, roll(total, GROUP), total)
+
+    def pack(tiles):
+        total = zero
+        for x, tile in enumerate(tiles):
+            total = total + roll(jnp.where(edge, tile, 0.0), GROUP * (x + H))
+        return to_strip(total)
+
+    def unpack(strip):
+        strip = jnp.where(high, roll(strip, -GROUP), strip)
+        return [jnp.where(edge, roll(strip, -GROUP * (x + H)), 0.0) for x in range(bx)]
+
+    def flat(ref, *at):
+        return ref.reshape(*ref.shape[:-3], ref.shape[-3] * ref.shape[-2], bz)
+
+    u_flat, t_flat, intact_flat = flat(u), flat(B["t", "field"]), flat(intact)
+    iy_flat = flat(B["iy"])
+
+    def clear(ref, depth):
+        zeros = jnp.zeros(ref.shape[2:], jnp.float32)
+
+        def body(i, carry):
+            for s in range(depth):
+                ref[s, i] = zeros
+            return carry
+
+        lax.fori_loop(0, ref.shape[1], body, 0)
+
+    def mask(ey, ez):
+        return B["mask"][PAIRS.index((ey, ez))]
+
+    def shift_main(name):
+        field, out = B[name, "field"], B[name, "main"]
+        for c in range(field.shape[0]):
+
+            def body(x, carry, c=c):
+                value = field[c, x + H, own, :]
+                for ez in range(1 - H, H + 1):
+                    moved = roll(value, -ez)
+                    out[ez + H, c, x, own, :] = moved
+                    out[ez + H, c, x, 0:PAD, :] = moved[0:PAD]
+                    out[ez + H, c, x, PAD + by :, :] = moved[0:PAD]
+                return carry
+
+            lax.fori_loop(0, bx, body, 0)
+
+    load_u.wait()
+    for c in range(3):
+        B["u", "in"][c] = pack([u[c, x + H, own, :] for x in range(bx)])
+    pl.semaphore_wait(barrier, count)
+
+    def spread(name):
+        field, strip = B[name, "field"], B[name, "in"]
+        sent = []
+        for d in sorted(everyone, key=lambda d: -sum(map(abs, d))):
+            if d[2]:
+                src = strip.at[:, edge_of(d[1], by, 0), :]
+            else:
+                src = field.at[:, edge_of(d[0], bx, H), edge_of(d[1], by, PAD), :]
+            sent.append(Shift(d, src, landing(name, minus(d))))
+        return sent
+
+    sent_u = spread("u")
+    load.wait()
+    sent_i = []
+    for (ex, ey), (k0, k1) in RUNS.items():
+        toward = 1 if ey > 0 else -1
+        at = slice(by - ey, by) if ey > 0 else slice(0, -ey)
+        sent_i.append(
+            Shift((0, toward, 0), intact.at[k0:k1, 0 : bx - ex, at, :], B["iy"].at[k0:k1, ex:, at, :])
+        )
+        if ex:
+            sent_i.append(
+                Shift((1, toward, 0), intact.at[k0:k1, bx - ex :, at, :], B["iy"].at[k0:k1, 0:ex, at, :])
+            )
+    for ex in range(1, H + 1):
+        k0, k1 = FIRST[ex], LAST[ex]
+        sent_i.append(Shift((1, 0, 0), intact.at[k0:k1, bx - ex :, :, :], B["ix"].at[k0:k1, 0:ex, own, :]))
+
+    beyond_x = number(has["gx", 1])
+    z_up, z_down = number(has["gz", 1]), number(has["gz", -1])
+
+    def slots_body(x, totals):
+        new = []
+        crossing = jnp.where(has["gx", 1], 1.0, 0.0)
+        for (ex, ey, az), total in zip(SLOTS, totals):
+            value = jnp.where(lane >= bz - az, intact[NUMBER[ex, ey, az], x].astype(jnp.float32) * z_up, 0.0)
+            if (ex, ey, -az) in NUMBER:
+                other = intact[NUMBER[ex, ey, -az], x].astype(jnp.float32) * z_down
+                value = jnp.where(lane < az, other, value)
+            if ex:
+                value = value * jnp.where(x + ex < bx, 1.0, crossing)
+            new.append(total + pltpu.roll(value, GROUP * (x + H), 1))
+        return tuple(new)
+
+    totals = lax.fori_loop(0, bx, slots_body, tuple(zero for _ in SLOTS))
+    y_inside = {}
+    for ey in range(-H, H + 1):
+        inside = (row + ey >= 0) & (row + ey < by)
+        y_inside[ey] = jnp.where(inside, 1.0, number(has["gy", 1 if ey > 0 else -1])) if ey else None
+    for (ex, ey, az), total in zip(SLOTS, totals):
+        value = to_strip(total) * terms(NUMBER[ex, ey, az])[0]
+        B["own_slots"][SLOT[ex, ey, az]] = value * y_inside[ey] if ey else value
+
+    for e, part, way in reversed(slot_moves):
+        sent_i.append(Shift(e, B["own_slots"].at[part, SENT[way], :], slot_landing(e, part, way)))
+
     for d in everyone:
 
         @pl.when(jnp.logical_not(exists[d]))
@@ -243,151 +365,33 @@
                 if ex and d == (-1, back, 0):
                     nothing(B["iy"].at[k0:k1, 0:ex, at, :])
 
-    lane = lax.broadcasted_iota(jnp.int32, (by, bz), 1)
-    row = lax.broadcasted_iota(jnp.int32, (by, bz), 0)
-    spot = lax.rem(lane, GROUP)
-    high = spot >= GROUP // 2
-    edge = (lane < H) | (lane >= bz - H)
-    inner = (lane >= H * GROUP) & (lane < (H + bx) * GROUP)
-    zero = jnp.zeros((by, bz), jnp.float32)
-
-    def number(condition):
-        return jnp.where(condition, 1.0, 0.0)
-
-    def roll(value, amount):
-        return pltpu.roll(value, amount % bz, 1) if amount % bz else value
-
-    def to_strip(total):
-        return jnp.where(high, roll(total, GROUP), total)
-
-    def pack(tiles):
-        total = zero
-        for x, tile in enumerate(tiles):
-            total = total + roll(jnp.where(edge, tile, 0.0), GROUP * (x + H))
-        return to_strip(total)
-
-    def unpack(strip):
-        strip = jnp.where(high, roll(strip, -GROUP), strip)
-        return [jnp.where(edge, roll(strip, -GROUP * (x + H)), 0.0) for x in range(bx)]
-
-    def flat(ref, *at):
-        return ref.reshape(*ref.shape[:-3], ref.shape[-3] * ref.shape[-2], bz)
-
-    u_flat, t_flat, intact_flat = flat(u), flat(B["t", "field"]), flat(intact)
-    iy_flat = flat(B["iy"])
-
-    def clear(ref, depth):
-        zeros = jnp.zeros(ref.shape[2:], jnp.float32)
-
-        def body(i, carry):
-            for s in range(depth):
-                ref[s, i] = zeros
-            return carry
-
-        lax.fori_loop(0, ref.shape[1], body, 0)
-
-    for name in ("u", "t"):
-        main, beside = B[name, "main"], B[name, "x"]
-        for c in range(main.shape[1]):
-            for s in range(7):
-
-                def blank(i, carry, s=s, c=c, main=main):
-                    main[s, c, i] = jnp.zeros((rows, bz), jnp.float32)
-                    return carry
-
-                lax.fori_loop(0, bx + H, blank, 0)
-
-                def blank_x(i, carry, s=s, c=c, beside=beside):
-                    beside[s, c, i] = jnp.zeros((rows, bz), jnp.float32)
-                    return carry
-
-                lax.fori_loop(0, 2 * H, blank_x, 0)
-    clear(B["t", "sums"], 7)
-    clear(B["u", "sums"], 7)
-
     for i, (ey, ez) in enumerate(PAIRS):
         B["mask"][i] = number((row + ey >= 0) & (row + ey < by) & (lane + ez >= 0) & (lane + ez < bz))
     for ez in range(-H, H + 1):
         B["lanes"][ez + H] = number((lane + ez >= 0) & (lane + ez < bz))
 
-    def mask(ey, ez):
-        return B["mask"][PAIRS.index((ey, ez))]
-
-    def shift_main(name):
-        field, out = B[name, "field"], B[name, "main"]
-        for c in range(field.shape[0]):
-
-            def body(x, carry, c=c):
-                value = field[c, x + H, own, :]
-                for ez in range(-H, H + 1):
-                    out[ez + H, c, x, own, :] = roll(value, -ez)
-                return carry
-
-            lax.fori_loop(0, bx, body, 0)
-
-    load_u.wait()
-    for c in range(3):
-        B["u", "in"][c] = pack([u[c, x + H, own, :] for x in range(bx)])
-    load.wait()
-
-    beyond_x = number(has["gx", 1])
-    z_up, z_down = number(has["gz", 1]), number(has["gz", -1])
-
-    def slots_body(x, totals):
-        new = []
-        crossing = jnp.where(has["gx", 1], 1.0, 0.0)
-        for (ex, ey, az), total in zip(SLOTS, totals):
-            value = jnp.where(lane >= bz - az, intact[NUMBER[ex, ey, az], x].astype(jnp.float32) * z_up, 0.0)
-            if (ex, ey, -az) in NUMBER:
-                other = intact[NUMBER[ex, ey, -az], x].astype(jnp.float32) * z_down
-                value = jnp.where(lane < az, other, value)
-            if ex:
-                value = value * jnp.where(x + ex < bx, 1.0, crossing)
-            new.append(total + pltpu.roll(value, GROUP * (x + H), 1))
-        return tuple(new)
-
-    totals = lax.fori_loop(0, bx, slots_body, tuple(zero for _ in SLOTS))
-    y_inside = {}
-    for ey in range(-H, H + 1):
-        inside = (row + ey >= 0) & (row + ey < by)
-        y_inside[ey] = jnp.where(inside, 1.0, number(has["gy", 1 if ey > 0 else -1])) if ey else None
-    for (ex, ey, az), total in zip(SLOTS, totals):
-        value = to_strip(total) * terms(NUMBER[ex, ey, az])[0]
-        B["own_slots"][SLOT[ex, ey, az]] = value * y_inside[ey] if ey else value
-
-    pl.semaphore_wait(barrier, count)
-
-    def spread(name, far=False):
-        field, strip = B[name, "field"], B[name, "in"]
-        sent = []
-        for d in sorted(everyone, key=lambda d: -sum(map(abs, d))):
-            if d[2]:
-                src = strip.at[:, edge_of(d[1], by, 0), :]
-            else:
-                src = field.at[:, edge_of(d[0], bx, H), edge_of(d[1], by, PAD), :]
-            sent.append(Shift(d, src, landing(name, minus(d))))
-        return sent
-
-    sent_u = spread("u")
-    sent_i = []
-    for (ex, ey), (k0, k1) in RUNS.items():
-        toward = 1 if ey > 0 else -1
-        at = slice(by - ey, by) if ey > 0 else slice(0, -ey)
-        if ex:
-            sent_i.append(
-                Shift((1, toward, 0), intact.at[k0:k1, bx - ex :, at, :], B["iy"].at[k0:k1, 0:ex, at, :])
-            )
-    for e, part, way in reversed(slot_moves):
-        sent_i.append(Shift(e, B["own_slots"].at[part, SENT[way], :], slot_landing(e, part, way)))
-    for (ex, ey), (k0, k1) in RUNS.items():
-        toward = 1 if ey > 0 else -1
-        at = slice(by - ey, by) if ey > 0 else slice(0, -ey)
-        sent_i.append(
-            Shift((0, toward, 0), intact.at[k0:k1, 0 : bx - ex, at, :], B["iy"].at[k0:k1, ex:, at, :])
-        )
-    for ex in range(1, H + 1):
-        k0, k1 = FIRST[ex], LAST[ex]
-        sent_i.append(Shift((1, 0, 0), intact.at[k0:k1, bx - ex :, :, :], B["ix"].at[k0:k1, 0:ex, own, :]))
+    def blank_rows(i, carry):
+        for name in ("u", "t"):
+            out = B[name, "x"]
+            for c in range(out.shape[1]):
+                for s in range(7):
+                    for part in (slice(0, PAD), slice(PAD + by, rows)):
+                        out[s, c, i, part, :] = jnp.zeros((PAD, bz), jnp.float32)
+        return carry
+
+    lax.fori_loop(0, 2 * H, blank_rows, 0)
+
+    def blank_planes(i, carry):
+        for name in ("u", "t"):
+            out = B[name, "main"]
+            for c in range(out.shape[1]):
+                for s in range(7):
+                    out[s, c, i] = jnp.zeros((rows, bz), jnp.float32)
+        return carry
+
+    lax.fori_loop(bx, bx + H, blank_planes, 0)
+    clear(B["t", "sums"], 7)
+    clear(B["u", "sums"], 7)
 
     shift_main("u")
 
@@ -465,28 +469,29 @@
         scale = j * lax.rsqrt(more * more * long2)
         return scale * p, scale * ext * q
 
-    def soften(x, carry):
-        for k in ORDER:
-            B["len"][k, x], B["ext"][k, x] = soften_one(B["jf"][k, x], B["ext"][k, x], B["len"][k, x], k)
-        return carry
-
-    lax.fori_loop(0, bx, soften, 0)
-
-    def beside(name):
-        field, z = B[name, "field"], B[name, "z"]
-        field_flat = u_flat if name == "u" else t_flat
-        comps = field.shape[0]
-        for c in range(comps):
+    NEEDED = (0, 2, 2, 2, 2, 0)
+
+    def beside_x(name):
+        field, out = B[name, "field"], B[name, "x"]
+        for c in range(field.shape[0]):
             for i in range(2 * H):
-                plane = i if i < H else i + bx
-                value = field[c, plane, own, :]
-                for ez in range(-H, H + 1):
-                    B[name, "x"][ez + H, c, i, own, :] = roll(value, -ez)
+                value = field[c, i if i < H else i + bx, own, :]
+                for ez in range(-NEEDED[i], NEEDED[i] + 1):
+                    out[ez + H, c, i, own, :] = roll(value, -ez)
+
+    def beside_y(name):
+        field_flat, out = flat(B[name, "field"]), B[name, "y"]
+        for c in range(out.shape[1]):
+            for i in range(2 * H):
                 at = PAD - H + i if i < H else PAD + by + i - H
                 for half in range(2):
                     value = field_flat[c, pl.ds(half * bx * rows + at, bx, stride=rows), :]
-                    for ez in range(-H, H + 1):
-                        B[name, "y"][ez + H, c, i, half * bx : half * bx + bx, :] = roll(value, -ez)
+                    for ez in range(-NEEDED[i], NEEDED[i] + 1):
+                        out[ez + H, c, i, half * bx : half * bx + bx, :] = roll(value, -ez)
+
+    def beside_z(name):
+        z, out = B[name, "z"], B[name, "q"]
+        for c in range(out.shape[1]):
             for tile in (slice(0, by), slice(by, rows)):
                 near, left, right = [jnp.where(high, z[0, i, c, tile, :], z[1, i, c, tile, :]) for i in (1, 0, 2)]
                 far = roll(jnp.where(lane < bz // 2 - GROUP, right, left), bx * GROUP)
@@ -494,11 +499,13 @@
                 for i, (ex, az) in enumerate(MOVES):
                     over = roll(value, GROUP - GROUP * ex - az)
                     under = roll(value, -GROUP - GROUP * ex + az)
-                    B[name, "q"][i, c, tile, :] = jnp.where(high, over, under)
-
-    for copy in sent_u:
-        copy.receive()
-    beside("u")
+                    out[i, c, tile, :] = jnp.where(high, over, under)
+
+    def receive(sent, kind):
+        for copy in sent:
+            dx, dy, dz = copy.direction
+            if ("z" if dz else "y" if dy else "x") == kind:
+                copy.receive()
 
     strip_sign = jnp.where(high, 1.0, -1.0)
 
@@ -523,12 +530,23 @@
     def bond(e):
         return NUMBER[e[2]] if e[0] == "z" and e[2] in NUMBER else bond_of(e[2])[0]
 
-    def stretch(part, total):
-        near, was = {}, None
+    def add(name, kind, at, totals):
+        base = B[name, "base"]
+        for c, total in enumerate(totals):
+            if kind == "x":
+                base[c, at] += total
+            else:
+                base_flat = flat(base)
+                base_flat[c, pl.ds(at, bx, stride=by), :] += total
+
+    def stretch(part):
+        near, was, total = {}, None, None
         for e in part:
             kind, at, step = e
             if (kind, at) != was:
-                was, near = (kind, at), {}
+                if was is not None:
+                    add("t", *was, [total])
+                was, near, total = (kind, at), {}, None
             i, k = place[e], bond(e)
             d = []
             for c in range(3):
@@ -547,7 +565,10 @@
             B["hext"][i] = ext
             B["hlen"][i] = long2
             term = B["hj"][i] * ext
-            total[kind, at] = total[kind, at] + term if (kind, at) in total else term
+            total = total + term if total is not None else term
+        if was[0] == "z":
+            return total
+        add("t", *was, [total])
 
     def from_slots(ex, ey, az):
         got, s = B["slots"], SLOT[ex, ey, az]
@@ -571,13 +592,21 @@
         value = iy_flat[k, pl.ds(from_row, bx, stride=by), :].astype(jnp.float32)
         return roll(value, ez) * (B["lanes"][step[2] + H] * terms(k)[0])
 
-    sums_t = {}
-    stretch([e for e in x_list + y_list if bond_of(e[2])[1]], sums_t)
-    for copy in sent_i:
-        copy.receive()
-    for e in x_list + y_list:
-        if not bond_of(e[2])[1]:
-            B["hj"][place[e]] = taken_flags(e)
+    own_x, taken_x = [[e for e in x_list if bond_of(e[2])[1] == mine] for mine in (True, False)]
+    own_y, taken_y = [[e for e in y_list if bond_of(e[2])[1] == mine] for mine in (True, False)]
+    receive(sent_u, "x")
+    beside_x("u")
+    stretch(own_x)
+    receive(sent_u, "y")
+    beside_y("u")
+    stretch(own_y)
+    receive(sent_u, "z")
+    beside_z("u")
+    receive(sent_i, "x")
+    for e in taken_x:
+        B["hj"][place[e]] = taken_flags(e)
+    stretch(taken_x)
+    receive(sent_i, "z")
     for e in z_list:
         ex, ey, az = e[2]
         value = B["own_slots"][SLOT[e[2]]] if e[2] in SLOT else None
@@ -585,20 +614,16 @@
             more = from_slots(-ex, -ey, az)
             value = more if value is None else value + more
         B["hj"][place[e]] = value
-    stretch([e for e in x_list + y_list if not bond_of(e[2])[1]], sums_t)
-    stretch(z_list, sums_t)
-
-    def finish(name, c, total, write):
+    strip_t = stretch(z_list)
+    receive(sent_i, "y")
+    for e in taken_y:
+        B["hj"][place[e]] = taken_flags(e)
+    stretch(taken_y)
+
+    def finish(name, c, strip, write):
         base = B[name, "base"]
-        base_flat = flat(base)
-        for r in range(by):
-            if ("y", r) in total:
-                base_flat[c, pl.ds(r, bx, stride=by), :] += total["y", r]
-        for x, strip in enumerate(unpack(total["z", 0])):
-            value = base[c, x] + strip
-            if ("x", x) in total:
-                value = value + total["x", x]
-            write(x, value)
+        for x, part in enumerate(unpack(strip)):
+            write(x, base[c, x] + part)
 
     t = B["t", "field"]
     own_theta = []
@@ -608,7 +633,7 @@
         t[0, x + H, own, :] = value
         own_theta.append(value)
 
-    finish("t", 0, sums_t, write_theta)
+    finish("t", 0, strip_t, write_theta)
     B["t", "in"][0] = pack(own_theta)
     sent_t = spread("t")
 
@@ -620,7 +645,8 @@
         for k in ORDER:
             ex, ey, ez = OFFSETS[k]
             part = slice(PAD + ey, PAD + ey + by)
-            scalar = B["len"][k, x] * (here + tz[ez + H, 0, x + ex, part, :]) + B["ext"][k, x]
+            both, alone = soften_one(B["jf"][k, x], B["ext"][k, x], B["len"][k, x], k)
+            scalar = both * (here + tz[ez + H, 0, x + ex, part, :]) + alone
             for c in range(3):
                 pushed = scalar * B["d"][k, x, c]
                 total[c] = total[c] + pushed
@@ -635,27 +661,42 @@
         i = place[e]
         B["hlen"][i], B["hext"][i] = soften_one(B["hj"][i], B["hext"][i], B["hlen"][i], bond(e))
 
-    for copy in sent_t:
-        copy.receive()
-    beside("t")
-    sums_f = [{}, {}, {}]
-    for e in everything:
-        kind, at, _ = e
-        i = place[e]
-        scalar = B["hlen"][i] * (inside("t", kind, at, 0) + other("t", e, 0)) + B["hext"][i]
-        for c in range(3):
-            pushed = scalar * B["hd"][i, c]
-            total = sums_f[c]
-            total[kind, at] = total[kind, at] + pushed if (kind, at) in total else pushed
+    for copy in copies:
+        copy.finish()
+
+    def forces(part):
+        was, total = None, None
+        for e in part:
+            kind, at, _ = e
+            if (kind, at) != was:
+                if was is not None:
+                    add("u", *was, total)
+                was, total = (kind, at), None
+                here = inside("t", kind, at, 0)
+            i = place[e]
+            scalar = B["hlen"][i] * (here + other("t", e, 0)) + B["hext"][i]
+            pushed = [scalar * B["hd"][i, c] for c in range(3)]
+            total = [total[c] + pushed[c] for c in range(3)] if total is not None else pushed
+        if was[0] == "z":
+            return total
+        add("u", *was, total)
+
+    receive(sent_t, "x")
+    beside_x("t")
+    forces(x_list)
+    receive(sent_t, "y")
+    beside_y("t")
+    forces(y_list)
+    receive(sent_t, "z")
+    beside_z("t")
+    strip_f = forces(z_list)
 
     for c in range(3):
 
         def write_force(x, value, c=c):
             force_out[c, x] = value
 
-        finish("u", c, sums_f[c], write_force)
-    for copy in copies:
-        copy.finish()
+        finish("u", c, strip_f[c], write_force)
 
 
 def shards(sizes, displacement, bond_intact):
@@ -677,7 +718,7 @@
         in_specs=[anywhere, anywhere],
         out_specs=(vmem, vmem),
         scratch_shapes=scratch,
-        compiler_params=pltpu.CompilerParams(collective_id=0, has_side_effects=True, vmem_limit_bytes=62000000),
+        compiler_params=pltpu.CompilerParams(collective_id=0, has_side_effects=True, vmem_limit_bytes=56375000),
     )(displacement, bond_intact)
 
 

time: 25.1 us -> 22.1 us (0.88)
  local copies, waits for them, and re-layouts: 2.91 us -> 1.26 us
  Pallas kernels: 21.3 us -> 20 us
    unnamed x2, local copies, waits for them, and re-layouts: 2.91 us -> 1.26 us
    pallas_call x1, Pallas kernels: 21.3 us -> 20 us  [shards(): pl.pallas_call(functools.partial(kernel, sizes, tuple(plan)), out_shape=(...]
where the time goes in v2:
time: 22.1 us; the launch traced here: 21.9 us
  Pallas kernels  20 us (90%)
  local copies, waits for them, and re-layouts  1.26 us (6%)
  between operations  0.64 us (3%)
    pallas_call x1, Pallas kernels, shards(): pl.pallas_call(functools.partial(kernel, sizes, tuple(plan)), out_shape=(...  20 us
    unnamed x2, local copies, waits for them, and re-layouts  1.26 us

profile of v2, /device:TPU:1, one launch (start us, length us, event | category | flops | bytes accessed | tf_op | source)
XLA Modules:
  0.0 21.9 jit_solution(15841250616641430536)
XLA Ops:
  0.6 20.0 %shard_map.41 = (f32[3,8,8,128]{3,2,1,0:T(8,128)S(1)}, f32[8,8,128]{2,1,0:T(8,128)S(1)}) custom-call(f32[3,8,8,128]{3,2,1,0:T(8,128)} %u_hbm.1, s32[61,8,8,128]{3,2,1,0:T(8,128)} %intact_hbm.1), custom_call_target="tpu_custom_call" | custom-call | tf_op jit(solution)/shard_map/pallas_call | solution.py:712
  20.7 0.6 %copy.6 = f32[3,8,8,128]{3,2,1,0:T(8,128)} copy(f32[3,8,8,128]{3,2,1,0:T(8,128)S(1)} %get-tuple-element.4) | data formatting | bytes 196608
  21.3 0.6 %copy.7 = f32[8,8,128]{2,1,0:T(8,128)} copy(f32[8,8,128]{2,1,0:T(8,128)S(1)} %get-tuple-element.5) | data formatting | bytes 65536

commit v3 on v2

--- a/solution.py
+++ b/solution.py
@@ -116,14 +116,15 @@
     plan["hd"] = (f, (halo, 3, by, bz))
     plan["mask"] = (f, (len(PAIRS), by, bz))
     plan["lanes"] = (f, (7, by, bz))
+    plan["scaled"] = (f, (bonds, by, bz))
     plan["ix"] = (i, (bonds, H, rows, bz))
     plan["iy"] = (i, (bonds, bx, by, bz))
     plan["own_slots"] = (f, (len(SLOTS), by, bz))
     plan["slots"] = (f, (2, 2, len(SLOTS), rows, bz))
     for name, c in (("u", 3), ("t", 1)):
         plan[name, "field"] = (f, (c, planes, rows, bz))
-        plan[name, "main"] = (f, (7, c, bx + H, rows, bz))
-        plan[name, "sums"] = (f, (7, bx + H, c, rows, bz))
+        plan[name, "main"] = (f, (7, c, bx, rows, bz))
+        plan[name, "sums"] = (f, (7, bx, c, rows, bz))
         plan[name, "base"] = (f, (c, bx, by, bz))
         plan[name, "x"] = (f, (7, c, 2 * H, rows, bz))
         plan[name, "y"] = (f, (7, c, 2 * H, planes, bz))
@@ -168,7 +169,7 @@
 
     barrier = pltpu.get_barrier_semaphore()
     count = jnp.int32(0)
-    for d in everyone:
+    for d in sorted(everyone, key=lambda d: -sum(map(abs, d))):
         count = count + jnp.where(exists[d], 1, 0).astype(jnp.int32)
 
         @pl.when(exists[d])
@@ -261,7 +262,7 @@
         zeros = jnp.zeros(ref.shape[2:], jnp.float32)
 
         def body(i, carry):
-            for s in range(depth):
+            for s in range(1, depth):
                 ref[s, i] = zeros
             return carry
 
@@ -272,22 +273,44 @@
 
     def shift_main(name):
         field, out = B[name, "field"], B[name, "main"]
-        for c in range(field.shape[0]):
-
-            def body(x, carry, c=c):
+
+        def body(x, carry):
+            for c in range(field.shape[0]):
                 value = field[c, x + H, own, :]
                 for ez in range(1 - H, H + 1):
                     moved = roll(value, -ez)
                     out[ez + H, c, x, own, :] = moved
                     out[ez + H, c, x, 0:PAD, :] = moved[0:PAD]
                     out[ez + H, c, x, PAD + by :, :] = moved[0:PAD]
-                return carry
-
-            lax.fori_loop(0, bx, body, 0)
+            return carry
+
+        lax.fori_loop(0, bx, body, 0)
+
+    for i, (ey, ez) in enumerate(PAIRS):
+        B["mask"][i] = number((row + ey >= 0) & (row + ey < by) & (lane + ez >= 0) & (lane + ez < bz))
+    for ez in range(-H, H + 1):
+        B["lanes"][ez + H] = number((lane + ez >= 0) & (lane + ez < bz))
+
+    def blank_rows(i, carry):
+        for name in ("u", "t"):
+            out = B[name, "x"]
+            for c in range(out.shape[1]):
+                for s in range(7):
+                    for part in (slice(0, PAD), slice(PAD + by, rows)):
+                        out[s, c, i, part, :] = jnp.zeros((PAD, bz), jnp.float32)
+        return carry
+
+    lax.fori_loop(0, 2 * H, blank_rows, 0)
+
+    clear(B["t", "sums"], 7)
+    clear(B["u", "sums"], 7)
+    for k, (ex, ey, ez) in enumerate(OFFSETS):
+        B["scaled"][k] = mask(ey, ez) * terms(k)[0]
 
     load_u.wait()
     for c in range(3):
         B["u", "in"][c] = pack([u[c, x + H, own, :] for x in range(bx)])
+    shift_main("u")
     pl.semaphore_wait(barrier, count)
 
     def spread(name):
@@ -356,7 +379,8 @@
                 if minus(e) == d:
                     nothing(slot_landing(e, part, way))
             if d == (-1, 0, 0):
-                nothing(B["ix"])
+                for ex in range(1, H + 1):
+                    nothing(B["ix"].at[FIRST[ex] : LAST[ex], 0:ex, own, :])
             for (ex, ey), (k0, k1) in RUNS.items():
                 back = -1 if ey > 0 else 1
                 at = slice(by - ey, by) if ey > 0 else slice(0, -ey)
@@ -365,44 +389,6 @@
                 if ex and d == (-1, back, 0):
                     nothing(B["iy"].at[k0:k1, 0:ex, at, :])
 
-    for i, (ey, ez) in enumerate(PAIRS):
-        B["mask"][i] = number((row + ey >= 0) & (row + ey < by) & (lane + ez >= 0) & (lane + ez < bz))
-    for ez in range(-H, H + 1):
-        B["lanes"][ez + H] = number((lane + ez >= 0) & (lane + ez < bz))
-
-    def blank_rows(i, carry):
-        for name in ("u", "t"):
-            out = B[name, "x"]
-            for c in range(out.shape[1]):
-                for s in range(7):
-                    for part in (slice(0, PAD), slice(PAD + by, rows)):
-                        out[s, c, i, part, :] = jnp.zeros((PAD, bz), jnp.float32)
-        return carry
-
-    lax.fori_loop(0, 2 * H, blank_rows, 0)
-
-    def blank_planes(i, carry):
-        for name in ("u", "t"):
-            out = B[name, "main"]
-            for c in range(out.shape[1]):
-                for s in range(7):
-                    out[s, c, i] = jnp.zeros((rows, bz), jnp.float32)
-        return carry
-
-    lax.fori_loop(bx, bx + H, blank_planes, 0)
-    clear(B["t", "sums"], 7)
-    clear(B["u", "sums"], 7)
-
-    shift_main("u")
-
-    def prepare(x, carry):
-        for k in ORDER:
-            ex, ey, ez = OFFSETS[k]
-            factor = jnp.where(x + ex < bx, terms(k)[0], 0.0) if ex else terms(k)[0]
-            B["jf"][k, x] = intact[k, x].astype(jnp.float32) * mask(ey, ez) * factor
-        return carry
-
-    lax.fori_loop(0, bx, prepare, 0)
 
     y_planes = {}
     for ex in range(H + 1):
@@ -412,7 +398,7 @@
         kind, at, step = e
         k, mine = bond_of(step)
         if kind == "x":
-            return intact[k, at].astype(jnp.float32) * mask(*step[1:]) * (terms(k)[0] * beyond_x)
+            return intact[k, at].astype(jnp.float32) * B["scaled"][k] * beyond_x
         value = intact_flat[k, pl.ds(at, bx, stride=by), :].astype(jnp.float32) * B["lanes"][step[2] + H]
         return value * (y_planes[step[0]] * (terms(k)[0] * number(has["gy", 1 if step[1] > 0 else -1])))
 
@@ -427,47 +413,51 @@
     acc_t, acc_f = B["t", "sums"], B["u", "sums"]
     uz, tz = B["u", "main"], B["t", "main"]
 
-    def dilate(x, carry):
+    groups = [[k for k in ORDER if OFFSETS[k][0] == ex] for ex in range(H + 1)]
+
+    def dilate(part, x, carry):
         mine = [u[c, x + H, own, :] for c in range(3)]
         near = [{v: mine[c] - float(v) if v else mine[c] for v in range(-H, H + 1)} for c in range(3)]
         total = zero
-        for k in ORDER:
+        for k in part:
             ex, ey, ez = OFFSETS[k]
-            part = slice(PAD + ey, PAD + ey + by)
-            d = [uz[ez + H, c, x + ex, part, :] - near[c][OFFSETS[k][c]] for c in range(3)]
+            at = slice(PAD + ey, PAD + ey + by)
+            d = [uz[ez + H, c, x + ex, at, :] - near[c][OFFSETS[k][c]] for c in range(3)]
             long2, ext = length(d, k)
-            term = B["jf"][k, x] * ext
+            flags = intact[k, x].astype(jnp.float32) * B["scaled"][k]
+            term = flags * ext
+            B["jf"][k, x] = flags
             for c in range(3):
                 B["d"][k, x, c] = d[c]
             B["ext"][k, x] = ext
             B["len"][k, x] = long2
             total = total + term
-            acc_t[ez + H, x + ex, 0, part, :] += term
-        B["t", "base"][0, x] = total
+            acc_t[ez + H, x + ex, 0, at, :] += term
+        B["t", "base"][0, x] = total if OFFSETS[part[0]][0] == 0 else B["t", "base"][0, x] + total
         return carry
 
-    lax.fori_loop(0, bx, dilate, 0)
+    for ex, part in enumerate(groups):
+        lax.fori_loop(0, bx - ex, functools.partial(dilate, part), 0)
 
     def gather(name):
         sums, base = B[name, "sums"], B[name, "base"]
-        for c in range(base.shape[0]):
-
-            def body(x, carry, c=c):
+
+        def body(x, carry):
+            for c in range(base.shape[0]):
                 value = base[c, x] + sums[H, x, c, own, :]
-                for ez in (-3, -2, -1, 1, 2, 3):
+                for ez in (-2, -1, 1, 2, 3):
                     value = value + roll(sums[ez + H, x, c, own, :], ez) * B["lanes"][H - ez]
                 base[c, x] = value
-                return carry
-
-            lax.fori_loop(0, bx, body, 0)
+            return carry
+
+        lax.fori_loop(0, bx, body, 0)
 
     gather("t")
 
     def soften_one(j, ext, long2, k):
         _, p, q = terms(k)
-        more = 1.0 + (ext * ext) * (1.0 / (radius_of(k) * soft_stretch) ** 2)
-        scale = j * lax.rsqrt(more * more * long2)
-        return scale * p, scale * ext * q
+        more = (ext * ext) * (1.0 / (radius_of(k) * soft_stretch) ** 2 / p) + 1.0 / p
+        return j * lax.rsqrt(more * more * long2), ext * (q / p)
 
     NEEDED = (0, 2, 2, 2, 2, 0)
 
@@ -639,23 +629,24 @@
 
     shift_main("t")
 
-    def push(x, carry):
+    def push(part, x, carry):
         here = t[0, x + H, own, :]
         total = [zero, zero, zero]
-        for k in ORDER:
+        for k in part:
             ex, ey, ez = OFFSETS[k]
-            part = slice(PAD + ey, PAD + ey + by)
-            both, alone = soften_one(B["jf"][k, x], B["ext"][k, x], B["len"][k, x], k)
-            scalar = both * (here + tz[ez + H, 0, x + ex, part, :]) + alone
+            at = slice(PAD + ey, PAD + ey + by)
+            g, h = soften_one(B["jf"][k, x], B["ext"][k, x], B["len"][k, x], k)
+            scalar = g * (here + tz[ez + H, 0, x + ex, at, :] + h)
             for c in range(3):
                 pushed = scalar * B["d"][k, x, c]
                 total[c] = total[c] + pushed
-                acc_f[ez + H, x + ex, c, part, :] -= pushed
+                acc_f[ez + H, x + ex, c, at, :] -= pushed
         for c in range(3):
-            B["u", "base"][c, x] = total[c]
+            B["u", "base"][c, x] = total[c] if OFFSETS[part[0]][0] == 0 else B["u", "base"][c, x] + total[c]
         return carry
 
-    lax.fori_loop(0, bx, push, 0)
+    for ex, part in enumerate(groups):
+        lax.fori_loop(0, bx - ex, functools.partial(push, part), 0)
     gather("u")
     for e in everything:
         i = place[e]
@@ -674,7 +665,7 @@
                 was, total = (kind, at), None
                 here = inside("t", kind, at, 0)
             i = place[e]
-            scalar = B["hlen"][i] * (here + other("t", e, 0)) + B["hext"][i]
+            scalar = B["hlen"][i] * (here + other("t", e, 0) + B["hext"][i])
             pushed = [scalar * B["hd"][i, c] for c in range(3)]
             total = [total[c] + pushed[c] for c in range(3)] if total is not None else pushed
         if was[0] == "z":

time: 22.1 us -> 20.9 us (0.946)
  Pallas kernels: 20 us -> 18.9 us
    pallas_call x1, Pallas kernels: 20 us -> 18.9 us  [shards(): pl.pallas_call(functools.partial(kernel, sizes, tuple(plan)), out_shape=(...]
where the time goes in v3:
time: 20.9 us; the launch traced here: 20.8 us
  Pallas kernels  18.9 us (90%)
  local copies, waits for them, and re-layouts  1.26 us (6%)
  between operations  0.64 us (3%)
    pallas_call x1, Pallas kernels, shards(): pl.pallas_call(functools.partial(kernel, sizes, tuple(plan)), out_shape=(...  18.9 us
    unnamed x2, local copies, waits for them, and re-layouts  1.26 us

profile of v3, /device:TPU:1, one launch (start us, length us, event | category | flops | bytes accessed | tf_op | source)
XLA Modules:
  0.0 20.8 jit_solution(11340508922556625009)
XLA Ops:
  0.6 18.9 %shard_map.41 = (f32[3,8,8,128]{3,2,1,0:T(8,128)S(1)}, f32[8,8,128]{2,1,0:T(8,128)S(1)}) custom-call(f32[3,8,8,128]{3,2,1,0:T(8,128)} %u_hbm.1, s32[61,8,8,128]{3,2,1,0:T(8,128)} %intact_hbm.1), custom_call_target="tpu_custom_call" | custom-call | tf_op jit(solution)/shard_map/pallas_call | solution.py:703
  19.5 0.6 %copy.6 = f32[3,8,8,128]{3,2,1,0:T(8,128)} copy(f32[3,8,8,128]{3,2,1,0:T(8,128)S(1)} %get-tuple-element.4) | data formatting | bytes 196608
  20.1 0.6 %copy.7 = f32[8,8,128]{2,1,0:T(8,128)} copy(f32[8,8,128]{2,1,0:T(8,128)S(1)} %get-tuple-element.5) | data formatting | bytes 65536

commit v4 on v3

--- a/solution.py
+++ b/solution.py
@@ -84,8 +84,20 @@
 MOVES = sorted({(s[0], s[2]) for s in STRIP})
 
 
+TILES = []
+WHERE = {}
+for _s in SLOTS:
+    _kind = (_s[1] > 0, _s[1] < 0, _s[0] > 0)
+    if TILES and len(TILES[-1][1]) == 1 and TILES[-1][0] == _kind:
+        WHERE[_s] = (len(TILES) - 1, True)
+        TILES[-1][1].append(_s)
+    else:
+        WHERE[_s] = (len(TILES), False)
+        TILES.append((_kind, [_s]))
+
+
 def span(test):
-    found = [i for i, s in enumerate(SLOTS) if test(s)]
+    found = [i for i, (_, pair) in enumerate(TILES) if test(pair[0])]
     assert found == list(range(found[0], found[-1] + 1))
     return slice(found[0], found[-1] + 1)
 
@@ -120,7 +132,8 @@
     plan["ix"] = (i, (bonds, H, rows, bz))
     plan["iy"] = (i, (bonds, bx, by, bz))
     plan["own_slots"] = (f, (len(SLOTS), by, bz))
-    plan["slots"] = (f, (2, 2, len(SLOTS), rows, bz))
+    plan["slots"] = (f, (2, 2, len(TILES), rows, bz))
+    plan["sent_slots"] = (f, (2, len(TILES), by, bz))
     for name, c in (("u", 3), ("t", 1)):
         plan[name, "field"] = (f, (c, planes, rows, bz))
         plan[name, "main"] = (f, (7, c, bx, rows, bz))
@@ -218,7 +231,7 @@
     x_all, x_up = span(lambda s: s[0] > 0), span(lambda s: s[0] > 0 and s[1] > 0)
     slot_moves = []
     for dz in (-1, 1):
-        for dx, parts in ((0, (slice(0, len(SLOTS)), up, down)), (1, (x_all, x_up, down))):
+        for dx, parts in ((0, (slice(0, len(TILES)), up, down)), (1, (x_all, x_up, down))):
             for way, dy in enumerate((0, 1, -1)):
                 slot_moves.append(((dx, dy, dz), parts[way], way))
 
@@ -286,60 +299,10 @@
 
         lax.fori_loop(0, bx, body, 0)
 
-    for i, (ey, ez) in enumerate(PAIRS):
-        B["mask"][i] = number((row + ey >= 0) & (row + ey < by) & (lane + ez >= 0) & (lane + ez < bz))
-    for ez in range(-H, H + 1):
-        B["lanes"][ez + H] = number((lane + ez >= 0) & (lane + ez < bz))
-
-    def blank_rows(i, carry):
-        for name in ("u", "t"):
-            out = B[name, "x"]
-            for c in range(out.shape[1]):
-                for s in range(7):
-                    for part in (slice(0, PAD), slice(PAD + by, rows)):
-                        out[s, c, i, part, :] = jnp.zeros((PAD, bz), jnp.float32)
-        return carry
-
-    lax.fori_loop(0, 2 * H, blank_rows, 0)
-
-    clear(B["t", "sums"], 7)
-    clear(B["u", "sums"], 7)
-    for k, (ex, ey, ez) in enumerate(OFFSETS):
-        B["scaled"][k] = mask(ey, ez) * terms(k)[0]
-
     load_u.wait()
     for c in range(3):
         B["u", "in"][c] = pack([u[c, x + H, own, :] for x in range(bx)])
-    shift_main("u")
-    pl.semaphore_wait(barrier, count)
-
-    def spread(name):
-        field, strip = B[name, "field"], B[name, "in"]
-        sent = []
-        for d in sorted(everyone, key=lambda d: -sum(map(abs, d))):
-            if d[2]:
-                src = strip.at[:, edge_of(d[1], by, 0), :]
-            else:
-                src = field.at[:, edge_of(d[0], bx, H), edge_of(d[1], by, PAD), :]
-            sent.append(Shift(d, src, landing(name, minus(d))))
-        return sent
-
-    sent_u = spread("u")
     load.wait()
-    sent_i = []
-    for (ex, ey), (k0, k1) in RUNS.items():
-        toward = 1 if ey > 0 else -1
-        at = slice(by - ey, by) if ey > 0 else slice(0, -ey)
-        sent_i.append(
-            Shift((0, toward, 0), intact.at[k0:k1, 0 : bx - ex, at, :], B["iy"].at[k0:k1, ex:, at, :])
-        )
-        if ex:
-            sent_i.append(
-                Shift((1, toward, 0), intact.at[k0:k1, bx - ex :, at, :], B["iy"].at[k0:k1, 0:ex, at, :])
-            )
-    for ex in range(1, H + 1):
-        k0, k1 = FIRST[ex], LAST[ex]
-        sent_i.append(Shift((1, 0, 0), intact.at[k0:k1, bx - ex :, :, :], B["ix"].at[k0:k1, 0:ex, own, :]))
 
     beyond_x = number(has["gx", 1])
     z_up, z_down = number(has["gz", 1]), number(has["gz", -1])
@@ -365,9 +328,44 @@
     for (ex, ey, az), total in zip(SLOTS, totals):
         value = to_strip(total) * terms(NUMBER[ex, ey, az])[0]
         B["own_slots"][SLOT[ex, ey, az]] = value * y_inside[ey] if ey else value
-
+    for i, (_, pair) in enumerate(TILES):
+        one = B["own_slots"][SLOT[pair[0]]]
+        for way, move in ((0, GROUP // 2), (1, -GROUP // 2)):
+            value = one
+            if len(pair) == 2:
+                two = roll(B["own_slots"][SLOT[pair[1]]], move)
+                value = jnp.where(high, one, two) if way else jnp.where(high, two, one)
+            B["sent_slots"][way, i] = value
+
+    pl.semaphore_wait(barrier, count)
+
+    def spread(name):
+        field, strip = B[name, "field"], B[name, "in"]
+        sent = []
+        for d in sorted(everyone, key=lambda d: -sum(map(abs, d))):
+            if d[2]:
+                src = strip.at[:, edge_of(d[1], by, 0), :]
+            else:
+                src = field.at[:, edge_of(d[0], bx, H), edge_of(d[1], by, PAD), :]
+            sent.append(Shift(d, src, landing(name, minus(d))))
+        return sent
+
+    sent_u = spread("u")
+    sent_i = []
+    ends = {g: (slice(by - g[1], by) if g[1] > 0 else slice(0, -g[1])) for g in RUNS}
+    for (ex, ey), (k0, k1) in RUNS.items():
+        src = intact.at[k0:k1, 0 : bx - ex, ends[ex, ey], :]
+        sent_i.append(Shift((0, 1 if ey > 0 else -1, 0), src, B["iy"].at[k0:k1, ex:, ends[ex, ey], :]))
     for e, part, way in reversed(slot_moves):
-        sent_i.append(Shift(e, B["own_slots"].at[part, SENT[way], :], slot_landing(e, part, way)))
+        sent_i.append(Shift(e, B["sent_slots"].at[(e[2] + 1) // 2, part, SENT[way], :], slot_landing(e, part, way)))
+    for (ex, ey), (k0, k1) in RUNS.items():
+        if ex:
+            src = intact.at[k0:k1, bx - ex :, ends[ex, ey], :]
+            sent_i.append(Shift((1, 1 if ey > 0 else -1, 0), src, B["iy"].at[k0:k1, 0:ex, ends[ex, ey], :]))
+    for ex in range(1, H + 1):
+        k0, k1 = FIRST[ex], LAST[ex]
+        sent_i.append(Shift((1, 0, 0), intact.at[k0:k1, bx - ex :, :, :], B["ix"].at[k0:k1, 0:ex, own, :]))
+
 
     for d in everyone:
 
@@ -389,6 +387,29 @@
                 if ex and d == (-1, back, 0):
                     nothing(B["iy"].at[k0:k1, 0:ex, at, :])
 
+
+    for i, (ey, ez) in enumerate(PAIRS):
+        B["mask"][i] = number((row + ey >= 0) & (row + ey < by) & (lane + ez >= 0) & (lane + ez < bz))
+    for ez in range(-H, H + 1):
+        B["lanes"][ez + H] = number((lane + ez >= 0) & (lane + ez < bz))
+
+    def blank_rows(i, carry):
+        for name in ("u", "t"):
+            out = B[name, "x"]
+            for c in range(out.shape[1]):
+                for s in range(7):
+                    for part in (slice(0, PAD), slice(PAD + by, rows)):
+                        out[s, c, i, part, :] = jnp.zeros((PAD, bz), jnp.float32)
+        return carry
+
+    lax.fori_loop(0, 2 * H, blank_rows, 0)
+
+    clear(B["t", "sums"], 7)
+    clear(B["u", "sums"], 7)
+    for k, (ex, ey, ez) in enumerate(OFFSETS):
+        B["scaled"][k] = mask(ey, ez) * terms(k)[0]
+
+    shift_main("u")
 
     y_planes = {}
     for ex in range(H + 1):
@@ -529,12 +550,12 @@
                 base_flat = flat(base)
                 base_flat[c, pl.ds(at, bx, stride=by), :] += total
 
-    def stretch(part):
+    def stretch(part, flags_known):
         near, was, total = {}, None, None
         for e in part:
             kind, at, step = e
             if (kind, at) != was:
-                if was is not None:
+                if was is not None and flags_known:
                     add("t", *was, [total])
                 was, near, total = (kind, at), {}, None
             i, k = place[e], bond(e)
@@ -554,21 +575,37 @@
                 B["hd"][i, c] = d[c]
             B["hext"][i] = ext
             B["hlen"][i] = long2
-            term = B["hj"][i] * ext
+            if flags_known:
+                term = B["hj"][i] * ext
+                total = total + term if total is not None else term
+        if flags_known:
+            add("t", *was, [total])
+
+    def weigh(part, flags_of):
+        was, total = None, None
+        for e in part:
+            if e[:2] != was:
+                if was is not None:
+                    add("t", *was, [total])
+                was, total = e[:2], None
+            flags = flags_of(e)
+            B["hj"][place[e]] = flags
+            term = flags * B["hext"][place[e]]
             total = total + term if total is not None else term
         if was[0] == "z":
             return total
         add("t", *was, [total])
 
     def from_slots(ex, ey, az):
-        got, s = B["slots"], SLOT[ex, ey, az]
+        got, (s, second) = B["slots"], WHERE[ex, ey, az]
         part = slice(PAD - ey, PAD - ey + by)
-        value = jnp.where(high, got[0, 0, s, part, :], got[1, 0, s, part, :])
+        a, b, move = (1, 0, GROUP // 2) if second else (0, 1, 0)
+        value = jnp.where(high, got[a, 0, s, part, :], got[b, 0, s, part, :])
         if ex:
-            far = jnp.where(high, got[0, 1, s, part, :], got[1, 1, s, part, :])
+            far = jnp.where(high, got[a, 1, s, part, :], got[b, 1, s, part, :])
             value = jnp.where(inner, value, roll(far, bx * GROUP))
-        over = roll(value, GROUP + GROUP * ex - az)
-        under = roll(value, -GROUP + GROUP * ex + az)
+        over = roll(value, GROUP + GROUP * ex - az - move)
+        under = roll(value, -GROUP + GROUP * ex + az + move)
         return jnp.where(spot >= GROUP - az, over, jnp.where(spot < az, under, 0.0))
 
     def taken_flags(e):
@@ -584,31 +621,32 @@
 
     own_x, taken_x = [[e for e in x_list if bond_of(e[2])[1] == mine] for mine in (True, False)]
     own_y, taken_y = [[e for e in y_list if bond_of(e[2])[1] == mine] for mine in (True, False)]
-    receive(sent_u, "x")
-    beside_x("u")
-    stretch(own_x)
-    receive(sent_u, "y")
-    beside_y("u")
-    stretch(own_y)
-    receive(sent_u, "z")
-    beside_z("u")
-    receive(sent_i, "x")
-    for e in taken_x:
-        B["hj"][place[e]] = taken_flags(e)
-    stretch(taken_x)
-    receive(sent_i, "z")
-    for e in z_list:
+
+    def strip_flags(e):
         ex, ey, az = e[2]
         value = B["own_slots"][SLOT[e[2]]] if e[2] in SLOT else None
         if (-ex, -ey, az) in SLOT:
             more = from_slots(-ex, -ey, az)
             value = more if value is None else value + more
-        B["hj"][place[e]] = value
-    strip_t = stretch(z_list)
+        return value
+
+    receive(sent_u, "x")
+    beside_x("u")
+    stretch(own_x, True)
+    stretch(taken_x, False)
+    receive(sent_u, "y")
+    beside_y("u")
+    stretch(own_y, True)
+    stretch(taken_y, False)
+    receive(sent_u, "z")
+    beside_z("u")
+    stretch(z_list, False)
+    receive(sent_i, "x")
+    weigh(taken_x, taken_flags)
+    receive(sent_i, "z")
+    strip_t = weigh(z_list, strip_flags)
     receive(sent_i, "y")
-    for e in taken_y:
-        B["hj"][place[e]] = taken_flags(e)
-    stretch(taken_y)
+    weigh(taken_y, taken_flags)
 
     def finish(name, c, strip, write):
         base = B[name, "base"]
@@ -616,15 +654,13 @@
             write(x, base[c, x] + part)
 
     t = B["t", "field"]
-    own_theta = []
 
     def write_theta(x, value):
         theta_out[x] = value
         t[0, x + H, own, :] = value
-        own_theta.append(value)
-
+
+    B["t", "in"][0] = pack([B["t", "base"][0, x] for x in range(bx)]) + strip_t
     finish("t", 0, strip_t, write_theta)
-    B["t", "in"][0] = pack(own_theta)
     sent_t = spread("t")
 
     shift_main("t")

time: 20.9 us -> 20.4 us (0.976)
  Pallas kernels: 18.9 us -> 18.4 us
    pallas_call x1, Pallas kernels: 18.9 us -> 18.4 us  [shards(): pl.pallas_call(functools.partial(kernel, sizes, tuple(plan)), out_shape=(...]
where the time goes in v4:
time: 20.4 us; the launch traced here: 20.2 us
  Pallas kernels  18.4 us (90%)
  local copies, waits for them, and re-layouts  1.26 us (6%)
  between operations  0.64 us (3%)
    pallas_call x1, Pallas kernels, shards(): pl.pallas_call(functools.partial(kernel, sizes, tuple(plan)), out_shape=(...  18.4 us
    unnamed x2, local copies, waits for them, and re-layouts  1.26 us

profile of v4, /device:TPU:1, one launch (start us, length us, event | category | flops | bytes accessed | tf_op | source)
XLA Modules:
  0.0 20.2 jit_solution(18414395640077575522)
XLA Ops:
  0.6 18.4 %shard_map.41 = (f32[3,8,8,128]{3,2,1,0:T(8,128)S(1)}, f32[8,8,128]{2,1,0:T(8,128)S(1)}) custom-call(f32[3,8,8,128]{3,2,1,0:T(8,128)} %u_hbm.1, s32[61,8,8,128]{3,2,1,0:T(8,128)} %intact_hbm.1), custom_call_target="tpu_custom_call" | custom-call | tf_op jit(solution)/shard_map/pallas_call | solution.py:739
  19.0 0.6 %copy.6 = f32[3,8,8,128]{3,2,1,0:T(8,128)} copy(f32[3,8,8,128]{3,2,1,0:T(8,128)S(1)} %get-tuple-element.4) | data formatting | bytes 196608
  19.6 0.6 %copy.7 = f32[8,8,128]{2,1,0:T(8,128)} copy(f32[8,8,128]{2,1,0:T(8,128)S(1)} %get-tuple-element.5) | data formatting | bytes 65536

commit v5 on v4

--- a/solution.py
+++ b/solution.py
@@ -353,11 +353,11 @@
     sent_u = spread("u")
     sent_i = []
     ends = {g: (slice(by - g[1], by) if g[1] > 0 else slice(0, -g[1])) for g in RUNS}
+    for e, part, way in reversed(slot_moves):
+        sent_i.append(Shift(e, B["sent_slots"].at[(e[2] + 1) // 2, part, SENT[way], :], slot_landing(e, part, way)))
     for (ex, ey), (k0, k1) in RUNS.items():
         src = intact.at[k0:k1, 0 : bx - ex, ends[ex, ey], :]
         sent_i.append(Shift((0, 1 if ey > 0 else -1, 0), src, B["iy"].at[k0:k1, ex:, ends[ex, ey], :]))
-    for e, part, way in reversed(slot_moves):
-        sent_i.append(Shift(e, B["sent_slots"].at[(e[2] + 1) // 2, part, SENT[way], :], slot_landing(e, part, way)))
     for (ex, ey), (k0, k1) in RUNS.items():
         if ex:
             src = intact.at[k0:k1, bx - ex :, ends[ex, ey], :]

time: 20.4 us -> 19.9 us (0.975)
  Pallas kernels: 18.4 us -> 17.8 us
    pallas_call x1, Pallas kernels: 18.4 us -> 17.8 us  [shards(): pl.pallas_call(functools.partial(kernel, sizes, tuple(plan)), out_shape=(...]
where the time goes in v5:
time: 19.9 us; the launch traced here: 19.7 us
  Pallas kernels  17.8 us (89%)
  local copies, waits for them, and re-layouts  1.26 us (6%)
  between operations  0.64 us (3%)
    pallas_call x1, Pallas kernels, shards(): pl.pallas_call(functools.partial(kernel, sizes, tuple(plan)), out_shape=(...  17.8 us
    unnamed x2, local copies, waits for them, and re-layouts  1.26 us

profile of v5, /device:TPU:1, one launch (start us, length us, event | category | flops | bytes accessed | tf_op | source)
XLA Modules:
  0.0 19.7 jit_solution(5581329716170413976)
XLA Ops:
  0.6 17.8 %shard_map.41 = (f32[3,8,8,128]{3,2,1,0:T(8,128)S(1)}, f32[8,8,128]{2,1,0:T(8,128)S(1)}) custom-call(f32[3,8,8,128]{3,2,1,0:T(8,128)} %u_hbm.1, s32[61,8,8,128]{3,2,1,0:T(8,128)} %intact_hbm.1), custom_call_target="tpu_custom_call" | custom-call | tf_op jit(solution)/shard_map/pallas_call | solution.py:739
  18.5 0.6 %copy.6 = f32[3,8,8,128]{3,2,1,0:T(8,128)} copy(f32[3,8,8,128]{3,2,1,0:T(8,128)S(1)} %get-tuple-element.4) | data formatting | bytes 196608
  19.1 0.6 %copy.7 = f32[8,8,128]{2,1,0:T(8,128)} copy(f32[8,8,128]{2,1,0:T(8,128)S(1)} %get-tuple-element.5) | data formatting | bytes 65536
